TPU v7x, 32 devices: a whole 2x2x4 slice. The times are simulated.
32 devices in a mesh: tm: 4 (over y, x), gx: 8 (over z, core).
Axes of the slice: x: 2, y: 2, z: 4, core: 2. Of those that a mesh axis runs over, the one named last changes fastest.
Arguments:
- state: float32 [8, 32, 256, 128], P('tm', 'gx'), may hold values from -3 to 3
- start_field: float32 [32, 256, 128], P('gx'), may hold values from -3 to 3
- diffusivity: float32 [32, 256, 128], P('gx'), may hold values from 0.3 to 3
- time_weights: float32 [8], P('tm'), may hold values from 0.4 to 1
- shift_real: float32 [8], replicated, may hold values from 0.5 to 2, as said below
- shift_imag: float32 [8], replicated, may hold values from -1 to 1, as said below
Outputs:
- new_state: float32 [8, 32, 256, 128], P('tm', 'gx')
Inputs may be any that keep to these rules, and one draw needn't show every extreme that they name: `shift_real`: shift_real_k = shift_real_(8 - k) for k = 1 .. 7. `shift_imag`: shift_imag_0 = shift_imag_(4) = 0 and shift_imag_k = - shift_imag_(8 - k), so the eigenvalues come in conjugate pairs.
All inputs are finite; a program needn't handle non-finite values.
Results may differ from a plain program's by a relative error of at most 0.0003.
Values sent between devices are 32-bit elements; how exact they have to be, the bound alone decides.
No kernel may reach another device: no remote copies, remote signals or barrier semaphores. Data moves between devices by JAX's collectives and lax.ppermute only.
A program may use at most 64 MiB of HBM per device.

v0:
```python
import math

import jax
import jax.numpy as jnp
from jax import lax
from jax.sharding import PartitionSpec as P

SWEEPS = 12


cheb_centre = 1.0
cheb_half = 0.7


def padded_2(block, sides, width):
    for axis, dim in sides:
        count = lax.axis_size(axis)
        forward = [(i, i + 1) for i in range(count - 1)]
        backward = [(target, source) for source, target in forward]
        low = lax.ppermute(
            lax.slice_in_dim(block, block.shape[dim] - width, None, axis=dim), axis, forward
        )
        high = lax.ppermute(lax.slice_in_dim(block, 0, width, axis=dim), axis, backward)
        block = jnp.concatenate([low, block, high], axis=dim)
    return block


def shifted(value, axis, steps):
    count = lax.axis_size(axis)
    initial, last = (max(0, -steps), min(count, count - steps))
    return lax.ppermute(value, axis, [(source, source + steps) for source in range(initial, last)])


def along(core, axis, lower):
    length = core.shape[axis]
    zeros = jnp.zeros_like(lax.slice_in_dim(core, 0, 1, axis=axis))
    if lower:
        return jnp.concatenate([zeros, lax.slice_in_dim(core, 0, length - 1, axis=axis)], axis)
    return jnp.concatenate([lax.slice_in_dim(core, 1, length, axis=axis), zeros], axis)


def six_near(padded):
    core = padded[..., 1:-1, :, :]
    rank = core.ndim
    return (
        core,
        (
            padded[..., :-2, :, :],
            padded[..., 2:, :, :],
            along(core, rank - 2, True),
            along(core, rank - 2, False),
            along(core, rank - 1, True),
            along(core, rank - 1, False),
        ),
    )


def operate(padded, faces, diag_sum):
    core, near = six_near(padded)
    total = faces[0] * near[0]
    for which in range(1, 6):
        total = total + faces[which] * near[which]
    return diag_sum * core - total


def time_matrix(total_steps, sign):
    index = lax.iota(jnp.int32, total_steps)
    product = index[:, None] * index[None, :] % total_steps
    angle = product.astype(jnp.float32) * (2.0 * math.pi / total_steps)
    cosine = jnp.cos(angle)
    sine = jnp.sin(angle) * sign
    matrix = jnp.stack([jnp.stack([cosine, sine], -1), jnp.stack([-sine, cosine], -1)], 1)
    return matrix.reshape((2 * total_steps, 2 * total_steps))


def apply_time(field, sign):
    total_steps = field.shape[0]
    flat = field.reshape((2 * total_steps, -1))
    mixed = jnp.dot(
        time_matrix(total_steps, sign),
        flat,
        precision=lax.Precision.HIGHEST,
        preferred_element_type=jnp.float32,
    )
    return mixed.reshape(field.shape)


def forward_time(field):
    return apply_time(field, 1.0)


def inverse_time(field):
    return apply_time(field, -1.0)


def shards(state, start_field, diffusivity, time_weights, shift_real, shift_imag):
    local_steps = state.shape[0]
    total_steps = local_steps * lax.axis_size("tm")
    device = lax.axis_index("tm")
    stacked = jnp.concatenate([diffusivity[None], state], 0)
    padded = padded_2(stacked, (("gx", 1),), 1)
    kappa, near = six_near(padded[0])
    faces = [0.5 * (kappa + other) for other in near]
    diag_sum = faces[0]
    for which in range(1, 6):
        diag_sum = diag_sum + faces[which]
    carried = shifted(state[local_steps - 1], "tm", 1)
    first_prior = jnp.where(device == 0, start_field, carried)
    prior = jnp.concatenate([first_prior[None], state[: local_steps - 1]], 0)
    applied = operate(padded[1:], faces, diag_sum)
    residual = prior - state - (applied + state * state * state - state)
    weighted = time_weights[:, None, None, None] * residual
    field = jnp.stack([weighted, jnp.zeros_like(weighted)], 1)
    local_index = device * local_steps + lax.iota(jnp.int32, local_steps)
    spectral = forward_time(lax.all_to_all(field, "tm", split_axis=3, concat_axis=0, tiled=True))
    spectral = lax.all_to_all(spectral, "tm", split_axis=0, concat_axis=3, tiled=True)
    chooser = (local_index[:, None] == lax.iota(jnp.int32, total_steps)[None, :]).astype(
        jnp.float32
    )
    mode_real = jnp.dot(
        chooser, shift_real, precision=lax.Precision.HIGHEST, preferred_element_type=jnp.float32
    ).reshape((-1, 1, 1, 1))
    mode_imag = jnp.dot(
        chooser, shift_imag, precision=lax.Precision.HIGHEST, preferred_element_type=jnp.float32
    ).reshape((-1, 1, 1, 1))
    denom_real = mode_real + diag_sum
    magnitude = denom_real * denom_real + mode_imag * mode_imag
    inverse_real = denom_real / magnitude
    inverse_imag = -mode_imag / magnitude
    source_real = spectral[:, 0]
    source_imag = spectral[:, 1]
    solution = jnp.stack(
        [
            source_real * inverse_real - source_imag * inverse_imag,
            source_real * inverse_imag + source_imag * inverse_real,
        ],
        1,
    )

    def sweep(turn, current):
        omega = 1.0 / (
            cheb_centre
            + cheb_half * jnp.cos(math.pi * (2.0 * turn.astype(jnp.float32) + 1.0) / (2.0 * SWEEPS))
        )
        extended = padded_2(current, (("gx", 2),), 1)
        image = operate(extended, faces, diag_sum)
        answer_real = current[:, 0]
        answer_imag = current[:, 1]
        misfit_real = source_real - (
            mode_real * answer_real - mode_imag * answer_imag + image[:, 0]
        )
        misfit_imag = source_imag - (
            mode_real * answer_imag + mode_imag * answer_real + image[:, 1]
        )
        return jnp.stack(
            [
                answer_real + omega * (misfit_real * inverse_real - misfit_imag * inverse_imag),
                answer_imag + omega * (misfit_real * inverse_imag + misfit_imag * inverse_real),
            ],
            1,
        )

    solution = lax.fori_loop(0, SWEEPS, sweep, solution)
    back = inverse_time(lax.all_to_all(solution, "tm", split_axis=3, concat_axis=0, tiled=True))
    back = lax.all_to_all(back, "tm", split_axis=0, concat_axis=3, tiled=True)
    delta = back[:, 0] / (total_steps * time_weights[:, None, None, None])
    return state + delta


def solution(mesh):
    in_specs = (
        P("tm", "gx", None, None),
        P("gx", None, None),
        P("gx", None, None),
        P("tm"),
        P(),
        P(),
    )
    out_specs = P("tm", "gx", None, None)
    return jax.shard_map(shards, mesh=mesh, in_specs=in_specs, out_specs=out_specs, check_vma=False)
```

profile of v0, /device:TPU:16, one launch (start us, length us, event | category | flops | bytes accessed | tf_op | source)
XLA Modules:
  0.0 401.5 jit_solution(8984971837982444184)
XLA Ops:
  2.4 4.2 %collective-permute-start.2 = (f32[4,256,128]{2,0,1:T(4,128)}, f32[4,256,128]{2,0,1:T(4,128)}, u32[]{:S(2)}, u32[]{:S(2)}) collective-permute-start(f32[4,256,128]{2,0,1:T(4,128)} %bitcast.138), channel_id=1, source_target_pairs={{0,8},{8,16},{16,24},{1,9},{9,17},{17,25},{2,10},{10,18},{18,26},{... | collective-permute-start | bytes 1572872 | tf_op jit(solution)/shard_map/ppermute | solution.py:31
  11.1 3.6 collective-permute-start.4
  27.7 3.4 add_add_fusion
  33.2 3.9 fusion.40
  38.8 3.8 all-to-all-start
  43.1 24.6 %all-to-all-done = f32[2,2,4,256,128]{4,2,0,1,3:T(4,128)S(1)} async-done(((f32[2,2,4,256,128]{4,2,0,1,3:T(4,128)}), f32[2,2,4,256,128]{4,2,0,1,3:T(4,128)S(1)}, u32[]{:S(2)}, u32[]{:S(2)}) %all-to-all-start) | async-done | bytes 2097184 | tf_op jit(solution)/shard_map/all_to_all | solution.py:115
  76.4 3.7 all-to-all-start.1
  86.0 18.5 %all-to-all-done.1 = f32[8,2,4,64,128]{4,3,2,1,0:T(8,128)S(1)} async-done(((f32[8,2,4,64,128]{4,3,2,1,0:T(8,128)}), f32[8,2,4,64,128]{4,3,2,1,0:T(8,128)S(1)}, u32[]{:S(2)}, u32[]{:S(2)}) %all-to-all-start.1) | async-done | bytes 2097184 | tf_op jit(solution)/shard_map/all_to_all | solution.py:116
  107.0 225.2 %while.17 = (s32[]{:T(128)}, f32[2,2,4,256,128]{4,3,2,1,0:T(8,128)S(1)}, f32[2,4,256,128]{3,2,1,0:T(8,128)}, f32[2,1,1,1]{0,3,2,1:T(1,128)S(1)}, f32[2,1,1,1]{0,...) while((s32[]{:T(128)}, ...), condition=%wide.region_1.2_spmd.clone.clone, body=%wide.region_0.1_spmd.clone.clone.sunk | while | flops 16252937 | bytes 94683824 | solution.py:163
  117.0 3.8 collective-permute-done.1
  135.8 3.8 collective-permute-done.1
  154.5 3.8 collective-permute-done.1
  158.4 3.4 fusion.96
  173.3 3.8 collective-permute-done.1
  177.2 3.4 fusion.96
  192.0 3.8 collective-permute-done.1
  195.9 3.4 fusion.96
  210.8 3.8 collective-permute-done.1
  229.6 3.8 collective-permute-done.1
  233.5 3.4 fusion.96
  248.3 3.8 collective-permute-done.1
  252.2 3.4 fusion.96
  267.1 3.8 collective-permute-done.1
  271.0 3.4 fusion.96
  285.9 3.8 collective-permute-done.1
  289.8 3.4 fusion.96
  304.6 3.8 collective-permute-done.1
  323.4 3.8 collective-permute-done.1
  334.9 3.8 all-to-all-start.2
  339.0 23.5 %all-to-all-done.2 = f32[2,2,4,256,128]{4,2,1,0,3:T(4,128)S(1)} async-done(((f32[2,2,4,256,128]{4,2,1,0,3:T(4,128)}), f32[2,2,4,256,128]{4,2,1,0,3:T(4,128)S(1)}, u32[]{:S(2)}, u32[]{:S(2)}) %all-to-all-start.2) | async-done | bytes 2097184 | tf_op jit(solution)/shard_map/all_to_all | solution.py:164
  371.2 3.6 all-to-all-start.3
  374.8 24.3 %all-to-all-done.3 = f32[8,2,4,64,128]{4,3,2,1,0:T(8,128)S(1)} async-done(((f32[8,2,4,64,128]{4,3,2,1,0:T(8,128)}), f32[8,2,4,64,128]{4,3,2,1,0:T(8,128)S(1)}, u32[]{:S(2)}, u32[]{:S(2)}) %all-to-all-start.3) | async-done | bytes 2097184 | tf_op jit(solution)/shard_map/all_to_all | solution.py:165
  (441 shorter events, 207.1 us)
Async XLA Ops:
  0.0 80.4 %copy-start = (f32[8]{0:T(128)S(1)}, f32[8]{0:T(128)}, u32[]{:S(2)}) copy-start(f32[8]{0:T(128)} %param.13) | copy-start | bytes 100
  2.4 28.8 %collective-permute-start.2 = (f32[4,256,128]{2,0,1:T(4,128)}, f32[4,256,128]{2,0,1:T(4,128)}, u32[]{:S(2)}, u32[]{:S(2)}) collective-permute-start(f32[4,256,128]{2,0,1:T(4,128)} %bitcast.138), channel_id=1, source_target_pairs={{0,8},{8,16},{16,24},{1,9},{9,17},{17,25},{2,10},{10,18},{18,26},{... | collective-permute-start | bytes 1572872 | tf_op jit(solution)/shard_map/ppermute | solution.py:31
  9.2 16.5 %collective-permute-start.3 = (f32[3,1,256,128]{3,1,0,2:T(1,128)}, f32[3,1,256,128]{3,1,0,2:T(1,128)S(1)}, u32[]{:S(2)}, u32[]{:S(2)}) collective-permute-start(f32[3,1,256,128]{3,1,0,2:T(1,128)} %get-tuple-element.566), channel_id=1, source_target_pairs={{0,1},{1,2},{2,3},{3,4},{4,5},{5,6},{6,7},{8,9},{9,10},{10,11},{11... | collective-permute-start | bytes 1179656 | tf_op jit(solution)/shard_map/ppermute | solution.py:20
  11.1 14.6 %collective-permute-start.4 = (f32[3,1,256,128]{3,1,0,2:T(1,128)}, f32[3,1,256,128]{3,1,0,2:T(1,128)}, u32[]{:S(2)}, u32[]{:S(2)}) collective-permute-start(f32[3,1,256,128]{3,1,0,2:T(1,128)} %get-tuple-element.567), channel_id=1, source_target_pairs={{1,0},{2,1},{3,2},{4,3},{5,4},{6,5},{7,6},{9,8},{10,9},{11,10},{12... | collective-permute-start | bytes 1179656 | tf_op jit(solution)/shard_map/ppermute | solution.py:23
  38.8 28.9 %all-to-all-start = ((f32[2,2,4,256,128]{4,2,0,1,3:T(4,128)}), f32[2,2,4,256,128]{4,2,0,1,3:T(4,128)S(1)}, u32[]{:S(2)}, u32[]{:S(2)}) async-start(f32[2,2,4,256,128]{4,2,0,1,3:T(4,128)} %stack.76), calls=%async_computation | async-start | bytes 4194304 | tf_op jit(solution)/shard_map/all_to_all | solution.py:115
  76.4 28.2 %all-to-all-start.1 = ((f32[8,2,4,64,128]{4,3,2,1,0:T(8,128)}), f32[8,2,4,64,128]{4,3,2,1,0:T(8,128)S(1)}, u32[]{:S(2)}, u32[]{:S(2)}) async-start(f32[8,2,4,64,128]{4,3,2,1,0:T(8,128)} %copy.107), calls=%async_computation.1 | async-start | bytes 4194304 | tf_op jit(solution)/shard_map/all_to_all | solution.py:116
  108.1 8.9 %collective-permute-start = (f32[2,2,1,256,128]{4,3,2,1,0:T(8,128)}, f32[2,2,1,256,128]{4,3,2,1,0:T(8,128)}, u32[]{:S(2)}, u32[]{:S(2)}) collective-permute-start(f32[2,2,1,256,128]{4,3,2,1,0:T(8,128)} %get-tuple-element.694), channel_id=1, source_target_pairs={{1,0},{2,1},{3,2},{4,3},{5,4},{6,5},{7,6},{9,8},{10,9},{11,10},{12... | collective-permute-start | bytes 1572872 | tf_op jit(solution)/shard_map/while/body/eval_jaxpr/ppermute | solution.py:23
  110.0 10.8 %collective-permute-start.1 = (f32[2,2,1,256,128]{4,3,2,1,0:T(8,128)}, f32[2,2,1,256,128]{4,3,2,1,0:T(8,128)}, u32[]{:S(2)}, u32[]{:S(2)}) collective-permute-start(f32[2,2,1,256,128]{4,3,2,1,0:T(8,128)} %get-tuple-element.695), channel_id=1, source_target_pairs={{0,1},{1,2},{2,3},{3,4},{4,5},{5,6},{6,7},{8,9},{9,10},{10,11},{11... | collective-permute-start | bytes 1572872 | tf_op jit(solution)/shard_map/while/body/eval_jaxpr/ppermute | solution.py:20
  126.8 8.9 %collective-permute-start = (f32[2,2,1,256,128]{4,3,2,1,0:T(8,128)}, f32[2,2,1,256,128]{4,3,2,1,0:T(8,128)}, u32[]{:S(2)}, u32[]{:S(2)}) collective-permute-start(f32[2,2,1,256,128]{4,3,2,1,0:T(8,128)} %get-tuple-element.694), channel_id=1, source_target_pairs={{1,0},{2,1},{3,2},{4,3},{5,4},{6,5},{7,6},{9,8},{10,9},{11,10},{12... | collective-permute-start | bytes 1572872 | tf_op jit(solution)/shard_map/while/body/eval_jaxpr/ppermute | solution.py:23
  128.8 10.8 %collective-permute-start.1 = (f32[2,2,1,256,128]{4,3,2,1,0:T(8,128)}, f32[2,2,1,256,128]{4,3,2,1,0:T(8,128)}, u32[]{:S(2)}, u32[]{:S(2)}) collective-permute-start(f32[2,2,1,256,128]{4,3,2,1,0:T(8,128)} %get-tuple-element.695), channel_id=1, source_target_pairs={{0,1},{1,2},{2,3},{3,4},{4,5},{5,6},{6,7},{8,9},{9,10},{10,11},{11... | collective-permute-start | bytes 1572872 | tf_op jit(solution)/shard_map/while/body/eval_jaxpr/ppermute | solution.py:20
  145.6 8.9 %collective-permute-start = (f32[2,2,1,256,128]{4,3,2,1,0:T(8,128)}, f32[2,2,1,256,128]{4,3,2,1,0:T(8,128)}, u32[]{:S(2)}, u32[]{:S(2)}) collective-permute-start(f32[2,2,1,256,128]{4,3,2,1,0:T(8,128)} %get-tuple-element.694), channel_id=1, source_target_pairs={{1,0},{2,1},{3,2},{4,3},{5,4},{6,5},{7,6},{9,8},{10,9},{11,10},{12... | collective-permute-start | bytes 1572872 | tf_op jit(solution)/shard_map/while/body/eval_jaxpr/ppermute | solution.py:23
  147.5 10.8 %collective-permute-start.1 = (f32[2,2,1,256,128]{4,3,2,1,0:T(8,128)}, f32[2,2,1,256,128]{4,3,2,1,0:T(8,128)}, u32[]{:S(2)}, u32[]{:S(2)}) collective-permute-start(f32[2,2,1,256,128]{4,3,2,1,0:T(8,128)} %get-tuple-element.695), channel_id=1, source_target_pairs={{0,1},{1,2},{2,3},{3,4},{4,5},{5,6},{6,7},{8,9},{9,10},{10,11},{11... | collective-permute-start | bytes 1572872 | tf_op jit(solution)/shard_map/while/body/eval_jaxpr/ppermute | solution.py:20
  164.4 8.9 %collective-permute-start = (f32[2,2,1,256,128]{4,3,2,1,0:T(8,128)}, f32[2,2,1,256,128]{4,3,2,1,0:T(8,128)}, u32[]{:S(2)}, u32[]{:S(2)}) collective-permute-start(f32[2,2,1,256,128]{4,3,2,1,0:T(8,128)} %get-tuple-element.694), channel_id=1, source_target_pairs={{1,0},{2,1},{3,2},{4,3},{5,4},{6,5},{7,6},{9,8},{10,9},{11,10},{12... | collective-permute-start | bytes 1572872 | tf_op jit(solution)/shard_map/while/body/eval_jaxpr/ppermute | solution.py:23
  166.3 10.8 %collective-permute-start.1 = (f32[2,2,1,256,128]{4,3,2,1,0:T(8,128)}, f32[2,2,1,256,128]{4,3,2,1,0:T(8,128)}, u32[]{:S(2)}, u32[]{:S(2)}) collective-permute-start(f32[2,2,1,256,128]{4,3,2,1,0:T(8,128)} %get-tuple-element.695), channel_id=1, source_target_pairs={{0,1},{1,2},{2,3},{3,4},{4,5},{5,6},{6,7},{8,9},{9,10},{10,11},{11... | collective-permute-start | bytes 1572872 | tf_op jit(solution)/shard_map/while/body/eval_jaxpr/ppermute | solution.py:20
  183.1 8.9 %collective-permute-start = (f32[2,2,1,256,128]{4,3,2,1,0:T(8,128)}, f32[2,2,1,256,128]{4,3,2,1,0:T(8,128)}, u32[]{:S(2)}, u32[]{:S(2)}) collective-permute-start(f32[2,2,1,256,128]{4,3,2,1,0:T(8,128)} %get-tuple-element.694), channel_id=1, source_target_pairs={{1,0},{2,1},{3,2},{4,3},{5,4},{6,5},{7,6},{9,8},{10,9},{11,10},{12... | collective-permute-start | bytes 1572872 | tf_op jit(solution)/shard_map/while/body/eval_jaxpr/ppermute | solution.py:23
  185.1 10.8 %collective-permute-start.1 = (f32[2,2,1,256,128]{4,3,2,1,0:T(8,128)}, f32[2,2,1,256,128]{4,3,2,1,0:T(8,128)}, u32[]{:S(2)}, u32[]{:S(2)}) collective-permute-start(f32[2,2,1,256,128]{4,3,2,1,0:T(8,128)} %get-tuple-element.695), channel_id=1, source_target_pairs={{0,1},{1,2},{2,3},{3,4},{4,5},{5,6},{6,7},{8,9},{9,10},{10,11},{11... | collective-permute-start | bytes 1572872 | tf_op jit(solution)/shard_map/while/body/eval_jaxpr/ppermute | solution.py:20
  201.9 8.9 %collective-permute-start = (f32[2,2,1,256,128]{4,3,2,1,0:T(8,128)}, f32[2,2,1,256,128]{4,3,2,1,0:T(8,128)}, u32[]{:S(2)}, u32[]{:S(2)}) collective-permute-start(f32[2,2,1,256,128]{4,3,2,1,0:T(8,128)} %get-tuple-element.694), channel_id=1, source_target_pairs={{1,0},{2,1},{3,2},{4,3},{5,4},{6,5},{7,6},{9,8},{10,9},{11,10},{12... | collective-permute-start | bytes 1572872 | tf_op jit(solution)/shard_map/while/body/eval_jaxpr/ppermute | solution.py:23
  203.8 10.8 %collective-permute-start.1 = (f32[2,2,1,256,128]{4,3,2,1,0:T(8,128)}, f32[2,2,1,256,128]{4,3,2,1,0:T(8,128)}, u32[]{:S(2)}, u32[]{:S(2)}) collective-permute-start(f32[2,2,1,256,128]{4,3,2,1,0:T(8,128)} %get-tuple-element.695), channel_id=1, source_target_pairs={{0,1},{1,2},{2,3},{3,4},{4,5},{5,6},{6,7},{8,9},{9,10},{10,11},{11... | collective-permute-start | bytes 1572872 | tf_op jit(solution)/shard_map/while/body/eval_jaxpr/ppermute | solution.py:20
  220.7 8.9 %collective-permute-start = (f32[2,2,1,256,128]{4,3,2,1,0:T(8,128)}, f32[2,2,1,256,128]{4,3,2,1,0:T(8,128)}, u32[]{:S(2)}, u32[]{:S(2)}) collective-permute-start(f32[2,2,1,256,128]{4,3,2,1,0:T(8,128)} %get-tuple-element.694), channel_id=1, source_target_pairs={{1,0},{2,1},{3,2},{4,3},{5,4},{6,5},{7,6},{9,8},{10,9},{11,10},{12... | collective-permute-start | bytes 1572872 | tf_op jit(solution)/shard_map/while/body/eval_jaxpr/ppermute | solution.py:23
  222.6 10.8 %collective-permute-start.1 = (f32[2,2,1,256,128]{4,3,2,1,0:T(8,128)}, f32[2,2,1,256,128]{4,3,2,1,0:T(8,128)}, u32[]{:S(2)}, u32[]{:S(2)}) collective-permute-start(f32[2,2,1,256,128]{4,3,2,1,0:T(8,128)} %get-tuple-element.695), channel_id=1, source_target_pairs={{0,1},{1,2},{2,3},{3,4},{4,5},{5,6},{6,7},{8,9},{9,10},{10,11},{11... | collective-permute-start | bytes 1572872 | tf_op jit(solution)/shard_map/while/body/eval_jaxpr/ppermute | solution.py:20
  239.4 8.9 %collective-permute-start = (f32[2,2,1,256,128]{4,3,2,1,0:T(8,128)}, f32[2,2,1,256,128]{4,3,2,1,0:T(8,128)}, u32[]{:S(2)}, u32[]{:S(2)}) collective-permute-start(f32[2,2,1,256,128]{4,3,2,1,0:T(8,128)} %get-tuple-element.694), channel_id=1, source_target_pairs={{1,0},{2,1},{3,2},{4,3},{5,4},{6,5},{7,6},{9,8},{10,9},{11,10},{12... | collective-permute-start | bytes 1572872 | tf_op jit(solution)/shard_map/while/body/eval_jaxpr/ppermute | solution.py:23
  241.3 10.8 %collective-permute-start.1 = (f32[2,2,1,256,128]{4,3,2,1,0:T(8,128)}, f32[2,2,1,256,128]{4,3,2,1,0:T(8,128)}, u32[]{:S(2)}, u32[]{:S(2)}) collective-permute-start(f32[2,2,1,256,128]{4,3,2,1,0:T(8,128)} %get-tuple-element.695), channel_id=1, source_target_pairs={{0,1},{1,2},{2,3},{3,4},{4,5},{5,6},{6,7},{8,9},{9,10},{10,11},{11... | collective-permute-start | bytes 1572872 | tf_op jit(solution)/shard_map/while/body/eval_jaxpr/ppermute | solution.py:20
  258.2 8.9 %collective-permute-start = (f32[2,2,1,256,128]{4,3,2,1,0:T(8,128)}, f32[2,2,1,256,128]{4,3,2,1,0:T(8,128)}, u32[]{:S(2)}, u32[]{:S(2)}) collective-permute-start(f32[2,2,1,256,128]{4,3,2,1,0:T(8,128)} %get-tuple-element.694), channel_id=1, source_target_pairs={{1,0},{2,1},{3,2},{4,3},{5,4},{6,5},{7,6},{9,8},{10,9},{11,10},{12... | collective-permute-start | bytes 1572872 | tf_op jit(solution)/shard_map/while/body/eval_jaxpr/ppermute | solution.py:23
  260.1 10.8 %collective-permute-start.1 = (f32[2,2,1,256,128]{4,3,2,1,0:T(8,128)}, f32[2,2,1,256,128]{4,3,2,1,0:T(8,128)}, u32[]{:S(2)}, u32[]{:S(2)}) collective-permute-start(f32[2,2,1,256,128]{4,3,2,1,0:T(8,128)} %get-tuple-element.695), channel_id=1, source_target_pairs={{0,1},{1,2},{2,3},{3,4},{4,5},{5,6},{6,7},{8,9},{9,10},{10,11},{11... | collective-permute-start | bytes 1572872 | tf_op jit(solution)/shard_map/while/body/eval_jaxpr/ppermute | solution.py:20
  277.0 8.9 %collective-permute-start = (f32[2,2,1,256,128]{4,3,2,1,0:T(8,128)}, f32[2,2,1,256,128]{4,3,2,1,0:T(8,128)}, u32[]{:S(2)}, u32[]{:S(2)}) collective-permute-start(f32[2,2,1,256,128]{4,3,2,1,0:T(8,128)} %get-tuple-element.694), channel_id=1, source_target_pairs={{1,0},{2,1},{3,2},{4,3},{5,4},{6,5},{7,6},{9,8},{10,9},{11,10},{12... | collective-permute-start | bytes 1572872 | tf_op jit(solution)/shard_map/while/body/eval_jaxpr/ppermute | solution.py:23
  278.9 10.8 %collective-permute-start.1 = (f32[2,2,1,256,128]{4,3,2,1,0:T(8,128)}, f32[2,2,1,256,128]{4,3,2,1,0:T(8,128)}, u32[]{:S(2)}, u32[]{:S(2)}) collective-permute-start(f32[2,2,1,256,128]{4,3,2,1,0:T(8,128)} %get-tuple-element.695), channel_id=1, source_target_pairs={{0,1},{1,2},{2,3},{3,4},{4,5},{5,6},{6,7},{8,9},{9,10},{10,11},{11... | collective-permute-start | bytes 1572872 | tf_op jit(solution)/shard_map/while/body/eval_jaxpr/ppermute | solution.py:20
  295.7 8.9 %collective-permute-start = (f32[2,2,1,256,128]{4,3,2,1,0:T(8,128)}, f32[2,2,1,256,128]{4,3,2,1,0:T(8,128)}, u32[]{:S(2)}, u32[]{:S(2)}) collective-permute-start(f32[2,2,1,256,128]{4,3,2,1,0:T(8,128)} %get-tuple-element.694), channel_id=1, source_target_pairs={{1,0},{2,1},{3,2},{4,3},{5,4},{6,5},{7,6},{9,8},{10,9},{11,10},{12... | collective-permute-start | bytes 1572872 | tf_op jit(solution)/shard_map/while/body/eval_jaxpr/ppermute | solution.py:23
  297.6 10.8 %collective-permute-start.1 = (f32[2,2,1,256,128]{4,3,2,1,0:T(8,128)}, f32[2,2,1,256,128]{4,3,2,1,0:T(8,128)}, u32[]{:S(2)}, u32[]{:S(2)}) collective-permute-start(f32[2,2,1,256,128]{4,3,2,1,0:T(8,128)} %get-tuple-element.695), channel_id=1, source_target_pairs={{0,1},{1,2},{2,3},{3,4},{4,5},{5,6},{6,7},{8,9},{9,10},{10,11},{11... | collective-permute-start | bytes 1572872 | tf_op jit(solution)/shard_map/while/body/eval_jaxpr/ppermute | solution.py:20
  314.5 8.9 %collective-permute-start = (f32[2,2,1,256,128]{4,3,2,1,0:T(8,128)}, f32[2,2,1,256,128]{4,3,2,1,0:T(8,128)}, u32[]{:S(2)}, u32[]{:S(2)}) collective-permute-start(f32[2,2,1,256,128]{4,3,2,1,0:T(8,128)} %get-tuple-element.694), channel_id=1, source_target_pairs={{1,0},{2,1},{3,2},{4,3},{5,4},{6,5},{7,6},{9,8},{10,9},{11,10},{12... | collective-permute-start | bytes 1572872 | tf_op jit(solution)/shard_map/while/body/eval_jaxpr/ppermute | solution.py:23
  316.4 10.8 %collective-permute-start.1 = (f32[2,2,1,256,128]{4,3,2,1,0:T(8,128)}, f32[2,2,1,256,128]{4,3,2,1,0:T(8,128)}, u32[]{:S(2)}, u32[]{:S(2)}) collective-permute-start(f32[2,2,1,256,128]{4,3,2,1,0:T(8,128)} %get-tuple-element.695), channel_id=1, source_target_pairs={{0,1},{1,2},{2,3},{3,4},{4,5},{5,6},{6,7},{8,9},{9,10},{10,11},{11... | collective-permute-start | bytes 1572872 | tf_op jit(solution)/shard_map/while/body/eval_jaxpr/ppermute | solution.py:20
  334.9 27.6 %all-to-all-start.2 = ((f32[2,2,4,256,128]{4,2,1,0,3:T(4,128)}), f32[2,2,4,256,128]{4,2,1,0,3:T(4,128)S(1)}, u32[]{:S(2)}, u32[]{:S(2)}) async-start(f32[2,2,4,256,128]{4,2,1,0,3:T(4,128)} %copy.118), calls=%async_computation.2 | async-start | bytes 4194304 | tf_op jit(solution)/shard_map/all_to_all | solution.py:164
  371.2 28.0 %all-to-all-start.3 = ((f32[8,2,4,64,128]{4,3,2,1,0:T(8,128)}), f32[8,2,4,64,128]{4,3,2,1,0:T(8,128)S(1)}, u32[]{:S(2)}, u32[]{:S(2)}) async-start(f32[8,2,4,64,128]{4,3,2,1,0:T(8,128)} %copy.121), calls=%async_computation.3 | async-start | bytes 4194304 | tf_op jit(solution)/shard_map/all_to_all | solution.py:165
  (133 other events, 674.3 us)
where the time goes:
time: 404 us; the launch traced here: 402 us
  waiting for transfers between devices  152 us (38%)
  local copies, waits for them, and re-layouts  90 us (22%)
  starting transfers between devices  76.5 us (19%)
  other arithmetic  72.5 us (18%)
  matrix products  6.04 us (1%)
    ppermute x13, waiting for transfers between devices, padded_2(): lax.ppermute(lax.slice_in_dim(block, block.shape[dim] - width, None, axis...  45.9 us
    sub x12, other arithmetic, operate(): return diag_sum * core - total  40.3 us
    slice x26, local copies, waits for them, and re-layouts, along(): lax.slice_in_dim(core, 0, length - 1, axis=axis)  38.9 us
    ppermute x13, starting transfers between devices, padded_2(): lax.ppermute(lax.slice_in_dim(block, block.shape[dim] - width, None, axis...  30.8 us
    ppermute x13, starting transfers between devices, padded_2(): lax.ppermute(lax.slice_in_dim(block, 0, width, axis=dim), axis, backward)  26.6 us
    all_to_all x1, waiting for transfers between devices, shards(): lax.all_to_all(field, 'tm', split_axis=3, concat_axis=0, tiled=True)  24.6 us
    all_to_all x1, waiting for transfers between devices, shards(): back = lax.all_to_all(back, 'tm', split_axis=0, concat_axis=3, tiled=True)  24.3 us
    all_to_all x1, waiting for transfers between devices, shards(): lax.all_to_all(solution, 'tm', split_axis=3, concat_axis=0, tiled=True)  23.5 us
  transfers between devices with their start and end apart: 31, of which 28 were waited for; matrix products, arithmetic and copies ran while one was open for 16% of the time, Pallas kernels for 0%

commit v1 on v0

v1 whole, which is shorter than its diff:
```python
import functools
import math

import jax
import jax.numpy as jnp
import numpy as np
from jax import lax
from jax.experimental import pallas as pl
from jax.experimental.pallas import tpu as pltpu
from jax.sharding import PartitionSpec as P

SWEEPS = 12
DEPTH = 3
YHALO = 16
PAD = 8
GROUPS = 1

cheb_centre = 1.0
cheb_half = 0.7

VMEM = pl.BlockSpec(memory_space=pltpu.VMEM)
SMEM = pl.BlockSpec(memory_space=pltpu.SMEM)


def omegas():
    return [
        1.0
        / (cheb_centre + cheb_half * math.cos(math.pi * (2 * turn + 1) / (2 * SWEEPS)))
        for turn in range(SWEEPS)
    ]


def forward_table(total):
    time = np.arange(total)
    table = np.zeros((total, total))
    table[0] = 1.0
    table[1] = np.where(time % 2 == 0, 1.0, -1.0)
    for mode in range(1, total // 2):
        angle = 2.0 * np.pi * (mode * time % total) / total
        table[2 * mode] = np.cos(angle)
        table[2 * mode + 1] = -np.sin(angle)
    return table


def inverse_table(total):
    table = forward_table(total).T.copy()
    table[:, 2:] *= 2.0
    return table / total


def near_sum(w_ref, lead, coef_ref, plane, row, rows=8):
    lanes = w_ref.shape[-1]
    at = pl.ds(row, rows)
    below = pl.ds(row - 1, rows)
    above = pl.ds(row + 1, rows)
    core = w_ref[lead, plane, at, :]
    face = coef_ref[2, plane, at, :]
    total = coef_ref[0, plane, at, :] * w_ref[lead, plane - 1, at, :]
    total = total + coef_ref[0, plane + 1, at, :] * w_ref[lead, plane + 1, at, :]
    total = total + coef_ref[1, plane, at, :] * w_ref[lead, plane, below, :]
    total = total + coef_ref[1, plane, above, :] * w_ref[lead, plane, above, :]
    total = total + face * pltpu.roll(core, 1, 1)
    total = total + pltpu.roll(face * core, lanes - 1, 1)
    return core, total


def sweeps_on(buffers, coef_ref, w0_ref, inv_ref, first, block, chunks, w0_plane, w0_row):
    own = DEPTH + 1
    for step in range(DEPTH):
        omega = omegas()[first + step]
        source, target = buffers[step % 2], buffers[(step + 1) % 2]
        reach = DEPTH - 1 - step

        def one(plane, _):
            for chunk in chunks:
                row = PAD + 8 * chunk
                at = pl.ds(8 * chunk - w0_row, 8)
                core_a, sum_a = near_sum(source, 0, coef_ref, plane, row)
                core_b, sum_b = near_sum(source, 1, coef_ref, plane, row)
                cross = inv_ref[2, plane - w0_plane, at, :]
                term_a = inv_ref[0, plane - w0_plane, at, :] * sum_a - cross * sum_b
                term_b = inv_ref[1, plane - w0_plane, at, :] * sum_b + cross * sum_a
                target[0, plane, pl.ds(row, 8), :] = (1.0 - omega) * core_a + omega * (
                    w0_ref[0, plane - w0_plane, at, :] + term_a
                )
                target[1, plane, pl.ds(row, 8), :] = (1.0 - omega) * core_b + omega * (
                    w0_ref[1, plane - w0_plane, at, :] + term_b
                )
            return 0

        lax.fori_loop(own - reach, own + block + reach, one, 0)
    return buffers[DEPTH % 2]


def send_out(result, parity, own_ref, on_ref, off_ref, block, window):
    low, rows = window
    own = DEPTH + 1
    first_on = jnp.where(parity == 0, block - DEPTH, 0)
    first_off = jnp.where(parity == 0, 0, block - DEPTH)
    for which in range(2):
        for plane in range(block):
            own_ref[which, plane] = result[which, own + plane, pl.ds(PAD + low, rows), :]
        for plane in range(DEPTH):
            on_ref[which, plane] = result[which, own + first_on + plane, pl.ds(PAD + low, rows), :]
            off_ref[which, plane] = result[which, own + first_off + plane, pl.ds(PAD + low, rows), :]


def pack_kernel(chunk, weights_ref, state_ref, out_ref):
    step, plane = pl.program_id(0), pl.program_id(1)
    pieces, rows, lanes = out_ref.shape[0], out_ref.shape[3], out_ref.shape[4]
    length = state_ref.shape[2]
    for piece in range(pieces):
        low = piece * chunk - YHALO
        first, last = max(low, 0), min(low + rows, length)
        if first > low:
            out_ref[piece, 0, 0, pl.ds(0, first - low), :] = jnp.zeros((first - low, lanes), jnp.float32)
        if last < low + rows:
            out_ref[piece, 0, 0, pl.ds(last - low, low + rows - last), :] = jnp.zeros(
                (low + rows - last, lanes), jnp.float32
            )
        out_ref[piece, 0, 0, pl.ds(first - low, last - first), :] = state_ref[
            0, 0, pl.ds(first, last - first), :
        ]

    @pl.when(plane == 0)
    def _():
        for piece in range(pieces):
            out_ref[piece, 0, 0, pl.ds(0, 1), :] = jnp.full((1, lanes), weights_ref[step], jnp.float32)


def finish_kernel(total, weights_ref, state_ref, back_ref, out_ref):
    step = pl.program_id(0)
    pieces, chunk = back_ref.shape[0], back_ref.shape[3]
    weight = jnp.full((8, state_ref.shape[3]), weights_ref[step], jnp.float32)
    scale = (1.0 / weight)[:1]
    for piece in range(pieces):
        at = pl.ds(piece * chunk, chunk)
        out_ref[0, 0, at, :] = state_ref[0, 0, at, :] + back_ref[piece, 0, 0] * scale


def setup_kernel(
    window,
    parity_ref,
    table_ref,
    shift_real_ref,
    shift_imag_ref,
    state_own,
    state_on,
    state_off,
    fixed_own,
    fixed_on,
    fixed_off,
    own_ref,
    on_ref,
    off_ref,
    w0_ref,
    inv_ref,
    coef_ref,
    wide,
    fixed,
    diag,
    resid,
    start,
    inverse,
    buffer_a,
    buffer_b,
):
    pair = pl.program_id(0)
    total, block, rows, lanes = state_own.shape
    own = DEPTH + 1
    planes = block + 2 * own
    padded = rows + 2 * PAD
    parity = parity_ref[0]
    chunks = range(rows // 8)

    @pl.when(pair == 0)
    def _():
        first_on = jnp.where(parity == 0, own + block, 0)
        first_off = jnp.where(parity == 0, 0, own + block)
        blank = jnp.zeros((PAD, lanes), jnp.float32)

        def clear(plane, _):
            for ref in (wide, fixed, coef_ref, buffer_a, buffer_b):
                for lead in range(ref.shape[0]):
                    ref[lead, plane, pl.ds(0, PAD), :] = blank
                    ref[lead, plane, pl.ds(padded - PAD, PAD), :] = blank
            return 0

        lax.fori_loop(0, planes, clear, 0)
        body = pl.ds(PAD, rows)

        def place(plane, _):
            for lead in range(total):
                wide[lead, own + plane, body, :] = state_own[lead, plane]
                wide[lead, first_on + plane, body, :] = state_on[lead, plane]
                wide[lead, first_off + plane, body, :] = state_off[lead, plane]
            for lead in range(2):
                fixed[lead, own + plane, body, :] = fixed_own[lead, plane]
                fixed[lead, first_on + plane, body, :] = fixed_on[lead, plane]
                fixed[lead, first_off + plane, body, :] = fixed_off[lead, plane]
            return 0

        lax.fori_loop(0, block, place, 0)
        lane = lax.broadcasted_iota(jnp.int32, (8, lanes), 1)

        def faces(plane, _):
            for chunk in chunks:
                row = PAD + 8 * chunk
                at = pl.ds(row, 8)
                kappa = fixed[1, plane, at, :]
                coef_ref[0, plane, at, :] = 0.5 * (fixed[1, plane - 1, at, :] + kappa)
                coef_ref[1, plane, at, :] = 0.5 * (fixed[1, plane, pl.ds(row - 1, 8), :] + kappa)
                near = 0.5 * (pltpu.roll(kappa, 1, 1) + kappa)
                coef_ref[2, plane, at, :] = jnp.where(lane == 0, 0.0, near)
            return 0

        lax.fori_loop(1, planes, faces, 0)

        def residuals(plane, _):
            for chunk in chunks:
                row = PAD + 8 * chunk
                at = pl.ds(row, 8)
                kappa = fixed[1, plane, at, :]
                low = 0.5 * (kappa + jnp.where(lane == 0, 0.0, pltpu.roll(kappa, 1, 1)))
                high = 0.5 * (kappa + jnp.where(lane == lanes - 1, 0.0, pltpu.roll(kappa, lanes - 1, 1)))
                around = coef_ref[0, plane, at, :] + coef_ref[0, plane + 1, at, :]
                around = around + coef_ref[1, plane, at, :]
                around = around + coef_ref[1, plane, pl.ds(row + 1, 8), :]
                around = around + low + high
                diag[plane, pl.ds(8 * chunk, 8), :] = around
                for lead in range(total):
                    core, near = near_sum(wide, lead, coef_ref, plane, row)
                    if lead == 0:
                        prior = fixed[0, plane, at, :]
                    else:
                        prior = wide[lead - 1, plane, at, :]
                    value = prior - (around * core - near) - core * core * core
                    weight = state_own[lead, 0, pl.ds(0, 1), :]
                    resid[lead, plane, pl.ds(8 * chunk, 8), :] = value * weight
            return 0

        lax.fori_loop(1, planes - 1, residuals, 0)

    other = jnp.where(pair == 0, total // 2, pair)
    real_a = shift_real_ref[pair]
    real_b = shift_real_ref[other]
    imag = shift_imag_ref[pair]
    table_a = [table_ref[2 * pair, lead] for lead in range(total)]
    table_b = [table_ref[2 * pair + 1, lead] for lead in range(total)]

    def begin(plane, _):
        for chunk in chunks:
            at = pl.ds(8 * chunk, 8)
            inside = fixed[1, plane, pl.ds(PAD + 8 * chunk, 8), :] > 0.0
            around = diag[plane, at, :]
            denom_a = real_a + around
            denom_b = real_b + around
            scale_a = 1.0 / (denom_a * denom_a + imag * imag)
            scale_b = 1.0 / (denom_b * denom_b + imag * imag)
            inv_a = jnp.where(inside, denom_a * scale_a, 0.0)
            inv_b = jnp.where(inside, denom_b * scale_b, 0.0)
            cross = jnp.where(inside, -imag * scale_a, 0.0)
            value = resid[0, plane, at, :]
            spec_a = table_a[0] * value
            spec_b = table_b[0] * value
            for lead in range(1, total):
                value = resid[lead, plane, at, :]
                spec_a = spec_a + table_a[lead] * value
                spec_b = spec_b + table_b[lead] * value
            w_a = inv_a * spec_a - cross * spec_b
            w_b = inv_b * spec_b + cross * spec_a
            inverse[0, plane, at, :] = inv_a
            inverse[1, plane, at, :] = inv_b
            inverse[2, plane, at, :] = cross
            start[0, plane, at, :] = w_a
            start[1, plane, at, :] = w_b
            buffer_a[0, plane, pl.ds(PAD + 8 * chunk, 8), :] = w_a
            buffer_a[1, plane, pl.ds(PAD + 8 * chunk, 8), :] = w_b
        return 0

    lax.fori_loop(1, planes - 1, begin, 0)
    result = sweeps_on((buffer_a, buffer_b), coef_ref, start, inverse, 0, block, chunks, 0, 0)
    send_out(result, parity, own_ref, on_ref, off_ref, block, window)

    def keep(plane, _):
        for lead in range(2):
            w0_ref[lead, plane] = start[lead, plane + 2, pl.ds(8, rows - 16), :]
        for lead in range(3):
            inv_ref[lead, plane] = inverse[lead, plane + 2, pl.ds(8, rows - 16), :]
        return 0

    lax.fori_loop(0, planes - 4, keep, 0)


def load_in(parity, own_ref, on_ref, off_ref, buffer_a, block, window):
    low, rows = window
    own = DEPTH + 1
    at = pl.ds(PAD + low, rows)
    first_on = jnp.where(parity == 0, own + block, 1)
    first_off = jnp.where(parity == 0, 1, own + block)
    for which in range(2):
        for plane in range(block):
            buffer_a[which, own + plane, at, :] = own_ref[which, plane]
        for plane in range(DEPTH):
            buffer_a[which, first_on + plane, at, :] = on_ref[which, plane]
            buffer_a[which, first_off + plane, at, :] = off_ref[which, plane]


def clear_edges(buffers, rows):
    planes, lanes = buffers[0].shape[1], buffers[0].shape[3]
    blank = jnp.zeros((PAD + 16, lanes), jnp.float32)

    @pl.when(pl.program_id(0) == 0)
    def _():
        def clear(plane, _):
            for ref in buffers:
                for lead in range(2):
                    ref[lead, plane, pl.ds(0, PAD + 16), :] = blank
                    ref[lead, plane, pl.ds(rows + PAD - 16, PAD + 16), :] = blank
            return 0

        lax.fori_loop(0, planes, clear, 0)


def middle_kernel(
    first,
    window,
    next_window,
    parity_ref,
    coef_ref,
    own_in,
    on_in,
    off_in,
    w0_ref,
    inv_ref,
    own_ref,
    on_ref,
    off_ref,
    buffer_a,
    buffer_b,
):
    block = own_in.shape[1]
    rows = coef_ref.shape[2] - 2 * PAD
    parity = parity_ref[0]
    clear_edges((buffer_a, buffer_b), rows)
    load_in(parity, own_in, on_in, off_in, buffer_a, block, window)
    chunks = range(1, rows // 8 - 1)
    result = sweeps_on((buffer_a, buffer_b), coef_ref, w0_ref, inv_ref, first, block, chunks, 2, 8)
    send_out(result, parity, own_ref, on_ref, off_ref, block, next_window)


def last_kernel(
    first,
    window,
    parity_ref,
    table_ref,
    coef_ref,
    own_in,
    on_in,
    off_in,
    w0_ref,
    inv_ref,
    out_ref,
    buffer_a,
    buffer_b,
):
    pair = pl.program_id(0)
    block = own_in.shape[1]
    total, chunk_rows = out_ref.shape[0], out_ref.shape[2]
    rows = coef_ref.shape[2] - 2 * PAD
    clear_edges((buffer_a, buffer_b), rows)
    load_in(parity_ref[0], own_in, on_in, off_in, buffer_a, block, window)
    chunks = range(1, rows // 8 - 1)
    result = sweeps_on((buffer_a, buffer_b), coef_ref, w0_ref, inv_ref, first, block, chunks, 2, 8)
    own = DEPTH + 1

    def gather(keep):
        def one(plane, _):
            for chunk in range(chunk_rows // 8):
                at = pl.ds(8 * chunk, 8)
                row = pl.ds(PAD + YHALO + 8 * chunk, 8)
                w_a = result[0, own + plane, row, :]
                w_b = result[1, own + plane, row, :]
                for lead in range(total):
                    value = table_ref[lead, 2 * pair] * w_a + table_ref[lead, 2 * pair + 1] * w_b
                    if keep:
                        value = value + out_ref[lead, plane, at, :]
                    out_ref[lead, plane, at, :] = value
            return 0

        lax.fori_loop(0, block, one, 0)

    @pl.when(pair == 0)
    def _():
        gather(False)

    @pl.when(pair > 0)
    def _():
        gather(True)


def shards(state, start_field, diffusivity, time_weights, shift_real, shift_imag):
    steps, block, length, lanes = state.shape
    pieces = lax.axis_size("tm")
    slabs = lax.axis_size("gx")
    total = steps * pieces
    pairs = total // 2
    chunk = length // pieces
    rows = chunk + 2 * YHALO
    own = DEPTH + 1
    planes = block + 2 * own
    padded = rows + 2 * PAD
    f32 = jnp.float32
    device = lax.axis_index("tm")
    parity = (lax.axis_index("gx") % 2).astype(jnp.int32).reshape((1,))
    on_pairs = [(i, i ^ 1) for i in range(slabs)]
    off_pairs = []
    for i in range(1, slabs - 1, 2):
        off_pairs += [(i, i + 1), (i + 1, i)]

    def swap_on(value):
        return lax.ppermute(value, "gx", on_pairs)

    def swap_off(value):
        return lax.ppermute(value, "gx", off_pairs)

    plane_spec = pl.BlockSpec((1, 1, length, lanes), lambda i, j: (i, j, 0, 0))
    packed = pl.pallas_call(
        functools.partial(pack_kernel, chunk),
        grid=(steps, block),
        in_specs=[SMEM, plane_spec],
        out_specs=pl.BlockSpec((pieces, 1, 1, rows, lanes), lambda i, j: (0, i, j, 0, 0)),
        out_shape=jax.ShapeDtypeStruct((pieces, steps, block, rows, lanes), f32),
        name="pack",
    )(time_weights, state)
    mixed = lax.all_to_all(packed, "tm", split_axis=0, concat_axis=0, tiled=True)
    mixed = mixed.reshape((total, block, rows, lanes))

    fixed = jnp.pad(jnp.stack([start_field, diffusivity]), ((0, 0), (0, 0), (YHALO, YHALO), (0, 0)))
    fixed = lax.dynamic_slice_in_dim(fixed, device * chunk, rows, axis=2)
    fixed_off = swap_off(fixed)
    fixed_on = swap_on(fixed)
    mixed_off = swap_off(mixed)
    mixed_on = swap_on(mixed)

    def window_of(done):
        halo = SWEEPS - done
        low = (YHALO - halo) // 4 * 4
        return low, rows - 2 * low

    windows = [window_of(DEPTH * (i + 1)) for i in range(SWEEPS // DEPTH - 1)]

    def pair_spec(count, *rest):
        return pl.BlockSpec((count,) + rest, lambda i: (i,) + (0,) * len(rest))

    def traffic(window):
        low, size = window
        specs = [pair_spec(2, block, size, lanes)] + [pair_spec(2, DEPTH, size, lanes)] * 2
        shapes = [jax.ShapeDtypeStruct((total, block, size, lanes), f32)]
        shapes += [jax.ShapeDtypeStruct((total, DEPTH, size, lanes), f32)] * 2
        return specs, shapes

    kept_specs = [pair_spec(2, planes - 4, rows - 16, lanes), pair_spec(3, planes - 4, rows - 16, lanes)]
    kept_shapes = [
        jax.ShapeDtypeStruct((total, planes - 4, rows - 16, lanes), f32),
        jax.ShapeDtypeStruct((3 * pairs, planes - 4, rows - 16, lanes), f32),
    ]
    buffers = [pltpu.VMEM((2, planes, padded, lanes), f32)] * 2
    params = pltpu.CompilerParams(vmem_limit_bytes=48 * 1024 * 1024)

    specs, shapes = traffic(windows[0])
    own_w, on_w, off_w, w0, inverse, coefs = pl.pallas_call(
        functools.partial(setup_kernel, windows[0]),
        grid=(pairs,),
        in_specs=[SMEM] * 4 + [VMEM] * 6,
        out_specs=specs + kept_specs + [VMEM],
        out_shape=shapes + kept_shapes + [jax.ShapeDtypeStruct((3, planes, padded, lanes), f32)],
        scratch_shapes=[
            pltpu.VMEM((total, planes, padded, lanes), f32),
            pltpu.VMEM((2, planes, padded, lanes), f32),
            pltpu.VMEM((planes, rows, lanes), f32),
            pltpu.VMEM((total, planes, rows, lanes), f32),
            pltpu.VMEM((2, planes, rows, lanes), f32),
            pltpu.VMEM((3, planes, rows, lanes), f32),
        ]
        + buffers,
        compiler_params=params,
        name="setup",
    )(
        parity,
        jnp.asarray(forward_table(total), f32),
        shift_real,
        shift_imag,
        mixed,
        mixed_on,
        mixed_off,
        fixed,
        fixed_on,
        fixed_off,
    )
    for phase in range(1, SWEEPS // DEPTH):
        window = windows[phase - 1]
        off_in = swap_off(off_w)
        on_in = swap_on(on_w)
        in_specs = traffic(window)[0]
        if phase < SWEEPS // DEPTH - 1:
            specs, shapes = traffic(windows[phase])
            own_w, on_w, off_w = pl.pallas_call(
                functools.partial(middle_kernel, DEPTH * phase, window, windows[phase]),
                grid=(pairs,),
                in_specs=[SMEM, VMEM] + in_specs + kept_specs,
                out_specs=specs,
                out_shape=shapes,
                scratch_shapes=buffers,
                compiler_params=params,
                name=f"middle{phase}",
            )(parity, coefs, own_w, on_in, off_in, w0, inverse)
        else:
            delta = pl.pallas_call(
                functools.partial(last_kernel, DEPTH * phase, window),
                grid=(pairs,),
                in_specs=[SMEM, SMEM, VMEM] + in_specs + kept_specs,
                out_specs=VMEM,
                out_shape=jax.ShapeDtypeStruct((total, block, chunk, lanes), f32),
                scratch_shapes=buffers,
                compiler_params=params,
                name="last",
            )(
                parity,
                jnp.asarray(inverse_table(total), f32),
                coefs,
                own_w,
                on_in,
                off_in,
                w0,
                inverse,
            )
    back = lax.all_to_all(
        delta.reshape((pieces, steps, block, chunk, lanes)), "tm", split_axis=0, concat_axis=0, tiled=True
    )
    return pl.pallas_call(
        functools.partial(finish_kernel, total),
        grid=(steps, block),
        in_specs=[
            SMEM,
            plane_spec,
            pl.BlockSpec((pieces, 1, 1, chunk, lanes), lambda i, j: (0, i, j, 0, 0)),
        ],
        out_specs=plane_spec,
        out_shape=jax.ShapeDtypeStruct((steps, block, length, lanes), f32),
        name="finish",
    )(time_weights, state, back)


def solution(mesh):
    in_specs = (
        P("tm", "gx", None, None),
        P("gx", None, None),
        P("gx", None, None),
        P("tm"),
        P(),
        P(),
    )
    out_specs = P("tm", "gx", None, None)
    return jax.shard_map(shards, mesh=mesh, in_specs=in_specs, out_specs=out_specs, check_vma=False)
```

time: 404 us -> 189 us (0.47)
  waiting for transfers between devices: 152 us -> 59.6 us
  local copies, waits for them, and re-layouts: 90 us -> 2.25 us
  other arithmetic: 72.5 us -> 0.04 us
  Pallas kernels: 0 us -> 71.5 us
  starting transfers between devices: 76.5 us -> 13.3 us
  blocking collectives: 0 us -> 41.8 us
  matrix products: 6.04 us -> 0 us
    all_to_all x4 -> x0, waiting for transfers between devices: 90.9 us -> none  [the longest x1 24.6 us: shards(): lax.all_to_all(field, 'tm', split_axis=3, concat_axis=0, tiled=True)]
    pallas_call x0 -> x6, Pallas kernels: none -> 71.5 us  [the longest x2 24.6 us: shards(): pl.pallas_call(functools.partial(middle_kernel, DEPTH * phase, window, wi...]
    slice x41 -> x0, local copies, waits for them, and re-layouts: 55.2 us -> none  [the longest x26 38.9 us: along(): lax.slice_in_dim(core, 0, length - 1, axis=axis)]
    ppermute x27 -> x10, starting transfers between devices: 61.6 us -> 13.3 us  [the longest x5 10.8 us: swap_off(): return lax.ppermute(value, 'gx', off_pairs)]
    sub x13 -> x0, other arithmetic: 42.2 us -> none  [the longest x12 40.3 us: operate(): return diag_sum * core - total]
    all_to_all x0 -> x2, blocking collectives: none -> 41.8 us  [the longest x1 23.7 us: shards(): lax.all_to_all(packed, 'tm', split_axis=0, concat_axis=0, tiled=True)]
    add x27 -> x0, other arithmetic: 19.9 us -> none  [the longest x12 9.55 us: sweep(): answer_real + omega * (misfit_real * inverse_real - misfit_imag * inverse...]
    unnamed x68 -> x20, local copies, waits for them, and re-layouts: 17.9 us -> 2.25 us
  transfers between devices with their start and end apart: 31 -> 10, of which waited for: 28 -> 6; matrix products, arithmetic and copies ran while one was open for 16% -> 0% of each run, Pallas kernels for 0% -> 0%
where the time goes in v1:
time: 189 us
  Pallas kernels  71.5 us (38%)
  waiting for transfers between devices  59.6 us (32%)
  blocking collectives  41.8 us (22%)
  starting transfers between devices  13.3 us (7%)
  local copies, waits for them, and re-layouts  2.25 us (1%)
    ppermute x5, waiting for transfers between devices, swap_off(): return lax.ppermute(value, 'gx', off_pairs)  59.2 us
    pallas_call x2, Pallas kernels, shards(): pl.pallas_call(functools.partial(middle_kernel, DEPTH * phase, window, wi...  24.6 us
    all_to_all x1, blocking collectives, shards(): lax.all_to_all(packed, 'tm', split_axis=0, concat_axis=0, tiled=True)  23.7 us
    pallas_call x1, Pallas kernels, shards(): pl.pallas_call(functools.partial(setup_kernel, windows[0]), grid=(pairs,)...  23.6 us
    all_to_all x1, blocking collectives, shards(): lax.all_to_all(delta.reshape((pieces, steps, block, chunk, lanes)), 'tm',...  18.1 us
    pallas_call x1, Pallas kernels, shards(): pl.pallas_call(functools.partial(last_kernel, DEPTH * phase, window), gri...  12.3 us
    ppermute x5, starting transfers between devices, swap_off(): return lax.ppermute(value, 'gx', off_pairs)  10.8 us
    pallas_call x1, Pallas kernels, shards(): pl.pallas_call(functools.partial(finish_kernel, total), grid=(steps, bloc...  5.55 us
  transfers between devices with their start and end apart: 10, of which 6 were waited for; matrix products, arithmetic and copies ran while one was open for 0% of the time, Pallas kernels for 0%

profile of v1, /device:TPU:16, one launch (start us, length us, event | category | flops | bytes accessed | tf_op | source)
XLA Modules:
  0.0 188.7 jit_solution(4488315703589020796)
XLA Ops:
  0.0 5.4 %pack.1 = f32[4,2,4,96,128]{4,3,2,1,0:T(8,128)} custom-call(f32[2]{0:T(128)} %weights_ref.3, f32[2,4,256,128]{3,2,1,0:T(8,128)} %state_ref.3), custom_call_target="tpu_custom_call" | custom-call | tf_op jit(solution)/shard_map/pack/pallas_call | solution.py:428
  5.4 23.7 %all_to_all.10 = f32[4,2,4,96,128]{4,3,2,1,0:T(8,128)S(1)} all-to-all(f32[4,2,4,96,128]{4,3,2,1,0:T(8,128)} %pack.1), channel_id=1, replica_groups=mesh['tm'=4,'gx'=8] {'tm'}, dimensions={0} | all-to-all | bytes 3145728 | tf_op jit(solution)/shard_map/all_to_all | solution.py:436
  29.1 2.1 %collective-permute-start.1 = (f32[8,4,96,128]{3,2,1,0:T(8,128)S(1)}, f32[8,4,96,128]{3,2,1,0:T(8,128)}, u32[]{:S(2)}, u32[]{:S(2)}) collective-permute-start(f32[8,4,96,128]{3,2,1,0:T(8,128)S(1)} %bitcast.6), channel_id=1, source_target_pairs={{1,2},{2,1},{3,4},{4,3},{5,6},{6,5},{9,10},{10,9},{11,12},{12,11},... | collective-permute-start | bytes 4718600 | tf_op jit(solution)/shard_map/ppermute | solution.py:425
  31.2 1.7 collective-permute-start
  33.0 0.0 copy-done.8
  33.0 2.0 %collective-permute-start.3 = (f32[2,4,96,128]{3,2,1,0:T(8,128)S(1)}, f32[2,4,96,128]{3,2,1,0:T(8,128)S(1)}, u32[]{:S(2)}, u32[]{:S(2)}) collective-permute-start(f32[2,4,96,128]{3,2,1,0:T(8,128)S(1)} %fusion.1.fixed_own), channel_id=1, source_target_pairs={{1,2},{2,1},{3,4},{4,3},{5,6},{6,5},{9,10},{10,9},{11,12},{12,11},... | collective-permute-start | bytes 1179656 | tf_op jit(solution)/shard_map/ppermute | solution.py:425
  35.0 0.1 collective-permute-start.2
  35.1 20.1 %collective-permute-done.3.fixed_off = f32[2,4,96,128]{3,2,1,0:T(8,128)S(1)} collective-permute-done((f32[2,4,96,128]{3,2,1,0:T(8,128)S(1)}, f32[2,4,96,128]{3,2,1,0:T(8,128)S(1)}, u32[]{:S(2)}, u32[]{:S(2)}) %collective-permute-start.3) | collective-permute-done | bytes 393248 | tf_op jit(solution)/shard_map/ppermute | solution.py:425
  55.2 0.0 collective-permute-done.2.fixed_on
  55.2 0.0 collective-permute-done.1.state_off
  55.2 0.0 collective-permute-done.state_on
  55.3 23.6 %setup.1 = (f32[8,4,88,128]{3,2,1,0:T(8,128)S(1)}, f32[8,3,88,128]{3,2,1,0:T(8,128)S(1)}, f32[8,3,88,128]{3,2,1,0:T(8,128)S(1)}, f32[8,8,80,128]{3,2,1,0:T(8,128...) custom-call(s32[1]{0:T(128)} %bitcast.parity_ref, f32[8,8]{1,0:T(8,128)S(1)} %copy-done.4, f32[8]{0:T(128)S(1)} %copy-done.5, ...), custom_call_target="tpu_custom_call" | custom-call | tf_op jit(solution)/shard_map/setup/pallas_call | solution.py:472
  78.9 1.1 copy-done.1
  80.0 0.1 collective-permute-start.4
  80.2 2.3 %collective-permute-start.5 = (f32[8,3,88,128]{3,2,1,0:T(8,128)S(1)}, f32[8,3,88,128]{3,2,1,0:T(8,128)S(1)}, u32[]{:S(2)}, u32[]{:S(2)}) collective-permute-start(f32[8,3,88,128]{3,2,1,0:T(8,128)S(1)} %get-tuple-element.20), channel_id=1, source_target_pairs={{1,2},{2,1},{3,4},{4,3},{5,6},{6,5},{9,10},{10,9},{11,12},{12,11},... | collective-permute-start | bytes 3244040 | tf_op jit(solution)/shard_map/ppermute | solution.py:425
  82.5 0.2 collective-permute-done.4.on_in
  82.7 13.9 %collective-permute-done.5.off_in = f32[8,3,88,128]{3,2,1,0:T(8,128)S(1)} collective-permute-done((f32[8,3,88,128]{3,2,1,0:T(8,128)S(1)}, f32[8,3,88,128]{3,2,1,0:T(8,128)S(1)}, u32[]{:S(2)}, u32[]{:S(2)}) %collective-permute-start.5) | collective-permute-done | bytes 1081376 | tf_op jit(solution)/shard_map/ppermute | solution.py:425
  96.6 12.3 %middle1.1 = (f32[8,4,80,128]{3,2,1,0:T(8,128)S(1)}, f32[8,3,80,128]{3,2,1,0:T(8,128)S(1)}, f32[8,3,80,128]{3,2,1,0:T(8,128)S(1)}) custom-call(s32[1]{0:T(128)} %bitcast.parity_ref, f32[3,12,112,128]{3,2,1,0:T(8,128)} %get-tuple-element.17.coef_ref, f32[8,4,88,128]{3,2,1,0:T(8,128)} %copy-done.1, f32[8,3,88,128]{3,2,1,0:T(8,128)S(1)} %collective-permute-done.4.on_in, ...), custom_call_target="tpu_custom_call" | custom-call | tf_op jit(solution)/shard_map/middle1/pallas_call | solution.py:508
  108.9 1.1 copy-done.2
  110.0 0.4 collective-permute-start.6
  110.4 2.1 %collective-permute-start.7 = (f32[8,3,80,128]{3,2,1,0:T(8,128)S(1)}, f32[8,3,80,128]{3,2,1,0:T(8,128)S(1)}, u32[]{:S(2)}, u32[]{:S(2)}) collective-permute-start(f32[8,3,80,128]{3,2,1,0:T(8,128)S(1)} %get-tuple-element.25), channel_id=1, source_target_pairs={{1,2},{2,1},{3,4},{4,3},{5,6},{6,5},{9,10},{10,9},{11,12},{12,11},... | collective-permute-start | bytes 2949128 | tf_op jit(solution)/shard_map/ppermute | solution.py:425
  112.5 0.1 collective-permute-done.6.on_in
  112.6 13.2 %collective-permute-done.7.off_in = f32[8,3,80,128]{3,2,1,0:T(8,128)S(1)} collective-permute-done((f32[8,3,80,128]{3,2,1,0:T(8,128)S(1)}, f32[8,3,80,128]{3,2,1,0:T(8,128)S(1)}, u32[]{:S(2)}, u32[]{:S(2)}) %collective-permute-start.7) | collective-permute-done | bytes 983072 | tf_op jit(solution)/shard_map/ppermute | solution.py:425
  125.8 12.3 %middle2.1 = (f32[8,4,72,128]{3,2,1,0:T(8,128)S(1)}, f32[8,3,72,128]{3,2,1,0:T(8,128)S(1)}, f32[8,3,72,128]{3,2,1,0:T(8,128)S(1)}) custom-call(s32[1]{0:T(128)} %bitcast.parity_ref, f32[3,12,112,128]{3,2,1,0:T(8,128)} %get-tuple-element.17.coef_ref, f32[8,4,80,128]{3,2,1,0:T(8,128)} %copy-done.2, f32[8,3,80,128]{3,2,1,0:T(8,128)S(1)} %collective-permute-done.6.on_in, ...), custom_call_target="tpu_custom_call" | custom-call | tf_op jit(solution)/shard_map/middle2/pallas_call | solution.py:508
  138.1 0.2 collective-permute-start.8
  138.3 2.3 %collective-permute-start.9 = (f32[8,3,72,128]{3,2,1,0:T(8,128)S(1)}, f32[8,3,72,128]{3,2,1,0:T(8,128)S(1)}, u32[]{:S(2)}, u32[]{:S(2)}) collective-permute-start(f32[8,3,72,128]{3,2,1,0:T(8,128)S(1)} %get-tuple-element.28), channel_id=1, source_target_pairs={{1,2},{2,1},{3,4},{4,3},{5,6},{6,5},{9,10},{10,9},{11,12},{12,11},... | collective-permute-start | bytes 2654216 | tf_op jit(solution)/shard_map/ppermute | solution.py:425
  140.7 0.0 collective-permute-done.8.on_in
  140.7 12.0 %collective-permute-done.9.off_in = f32[8,3,72,128]{3,2,1,0:T(8,128)S(1)} collective-permute-done((f32[8,3,72,128]{3,2,1,0:T(8,128)S(1)}, f32[8,3,72,128]{3,2,1,0:T(8,128)S(1)}, u32[]{:S(2)}, u32[]{:S(2)}) %collective-permute-start.9) | collective-permute-done | bytes 884768 | tf_op jit(solution)/shard_map/ppermute | solution.py:425
  152.7 0.0 copy-done.3
  152.7 12.3 %last.1 = f32[8,4,64,128]{3,2,1,0:T(8,128)S(1)} custom-call(s32[1]{0:T(128)} %bitcast.parity_ref, f32[8,8]{1,0:T(8,128)S(1)} %copy-done.3, f32[3,12,112,128]{3,2,1,0:T(8,128)S(1)} %copy-done, f32[8,4,72,128]{3,2,1,0:T(8,128)S(1)} %get-tuple-element.26.own_in, f32[8,3,72,128]{3,2,1,0:T(8,128)S(1)} %collective-permute-done.8.on_in, ...), custom_call_target="tpu_custom_call" | custom-call | tf_op jit(solution)/shard_map/last/pallas_call | solution.py:519
  165.0 18.1 %all_to_all.11.back_ref = f32[4,2,4,64,128]{4,3,2,1,0:T(8,128)} all-to-all(f32[4,2,4,64,128]{4,3,2,1,0:T(8,128)S(1)} %bitcast.5), channel_id=1, replica_groups=mesh['tm'=4,'gx'=8] {'tm'}, dimensions={0} | all-to-all | bytes 2097152 | tf_op jit(solution)/shard_map/all_to_all | solution.py:538
  183.1 5.5 %finish.1 = f32[2,4,256,128]{3,2,1,0:T(8,128)} custom-call(f32[2]{0:T(128)} %weights_ref.3, f32[2,4,256,128]{3,2,1,0:T(8,128)} %state_ref.3, f32[4,2,4,64,128]{4,3,2,1,0:T(8,128)} %all_to_all.11.back_ref), custom_call_target="tpu_custom_call" | custom-call | tf_op jit(solution)/shard_map/finish/pallas_call | solution.py:541
  (17 shorter events, 0.1 us)
Async XLA Ops:
  5.4 27.5 %copy-start.8 = (f32[4,256,128]{2,1,0:T(8,128)S(1)}, f32[4,256,128]{2,1,0:T(8,128)}, u32[]{:S(2)}) copy-start(f32[4,256,128]{2,1,0:T(8,128)} %param.9) | copy-start | bytes 1572868
  5.4 27.5 %copy-start.9 = (f32[4,256,128]{2,1,0:T(8,128)S(1)}, f32[4,256,128]{2,1,0:T(8,128)}, u32[]{:S(2)}) copy-start(f32[4,256,128]{2,1,0:T(8,128)} %param.10) | copy-start | bytes 1572868
  29.1 26.1 %copy-start.7 = (f32[4,2,4,96,128]{4,3,2,1,0:T(8,128)}, f32[4,2,4,96,128]{4,3,2,1,0:T(8,128)S(1)}, u32[]{:S(2)}) copy-start(f32[4,2,4,96,128]{4,3,2,1,0:T(8,128)S(1)} %all_to_all.10) | copy-start | bytes 4718596
  29.1 26.1 %copy-start.4 = (f32[8,8]{1,0:T(8,128)S(1)}, f32[8,8]{1,0:T(8,128)}, u32[]{:S(2)}) copy-start(f32[8,8]{1,0:T(8,128)} %constant.32.clone.table_ref) | copy-start | bytes 772
  29.1 26.1 %copy-start.5 = (f32[8]{0:T(128)S(1)}, f32[8]{0:T(128)}, u32[]{:S(2)}) copy-start(f32[8]{0:T(128)} %shift_real_ref.1) | copy-start | bytes 100
  29.1 26.1 %copy-start.6 = (f32[8]{0:T(128)S(1)}, f32[8]{0:T(128)}, u32[]{:S(2)}) copy-start(f32[8]{0:T(128)} %shift_imag_ref.1) | copy-start | bytes 100
  29.1 26.1 %collective-permute-start.1 = (f32[8,4,96,128]{3,2,1,0:T(8,128)S(1)}, f32[8,4,96,128]{3,2,1,0:T(8,128)}, u32[]{:S(2)}, u32[]{:S(2)}) collective-permute-start(f32[8,4,96,128]{3,2,1,0:T(8,128)S(1)} %bitcast.6), channel_id=1, source_target_pairs={{1,2},{2,1},{3,4},{4,3},{5,6},{6,5},{9,10},{10,9},{11,12},{12,11},... | collective-permute-start | bytes 4718600 | tf_op jit(solution)/shard_map/ppermute | solution.py:425
  31.2 24.0 %collective-permute-start = (f32[8,4,96,128]{3,2,1,0:T(8,128)S(1)}, f32[8,4,96,128]{3,2,1,0:T(8,128)}, u32[]{:S(2)}, u32[]{:S(2)}) collective-permute-start(f32[8,4,96,128]{3,2,1,0:T(8,128)S(1)} %bitcast.7), channel_id=1, source_target_pairs={{0,1},{1,0},{2,3},{3,2},{4,5},{5,4},{6,7},{7,6},{8,9},{9,8},{10,11... | collective-permute-start | bytes 4718600 | tf_op jit(solution)/shard_map/ppermute | solution.py:422
  33.0 22.2 %collective-permute-start.3 = (f32[2,4,96,128]{3,2,1,0:T(8,128)S(1)}, f32[2,4,96,128]{3,2,1,0:T(8,128)S(1)}, u32[]{:S(2)}, u32[]{:S(2)}) collective-permute-start(f32[2,4,96,128]{3,2,1,0:T(8,128)S(1)} %fusion.1.fixed_own), channel_id=1, source_target_pairs={{1,2},{2,1},{3,4},{4,3},{5,6},{6,5},{9,10},{10,9},{11,12},{12,11},... | collective-permute-start | bytes 1179656 | tf_op jit(solution)/shard_map/ppermute | solution.py:425
  35.0 20.2 %collective-permute-start.2 = (f32[2,4,96,128]{3,2,1,0:T(8,128)S(1)}, f32[2,4,96,128]{3,2,1,0:T(8,128)S(1)}, u32[]{:S(2)}, u32[]{:S(2)}) collective-permute-start(f32[2,4,96,128]{3,2,1,0:T(8,128)S(1)} %fusion.1.fixed_own), channel_id=1, source_target_pairs={{0,1},{1,0},{2,3},{3,2},{4,5},{5,4},{6,7},{7,6},{8,9},{9,8},{10,11... | collective-permute-start | bytes 1179656 | tf_op jit(solution)/shard_map/ppermute | solution.py:422
  78.9 1.1 copy-start.1
  80.0 2.7 %collective-permute-start.4 = (f32[8,3,88,128]{3,2,1,0:T(8,128)S(1)}, f32[8,3,88,128]{3,2,1,0:T(8,128)S(1)}, u32[]{:S(2)}, u32[]{:S(2)}) collective-permute-start(f32[8,3,88,128]{3,2,1,0:T(8,128)S(1)} %get-tuple-element.19), channel_id=1, source_target_pairs={{0,1},{1,0},{2,3},{3,2},{4,5},{5,4},{6,7},{7,6},{8,9},{9,8},{10,11... | collective-permute-start | bytes 3244040 | tf_op jit(solution)/shard_map/ppermute | solution.py:422
  80.2 16.5 %collective-permute-start.5 = (f32[8,3,88,128]{3,2,1,0:T(8,128)S(1)}, f32[8,3,88,128]{3,2,1,0:T(8,128)S(1)}, u32[]{:S(2)}, u32[]{:S(2)}) collective-permute-start(f32[8,3,88,128]{3,2,1,0:T(8,128)S(1)} %get-tuple-element.20), channel_id=1, source_target_pairs={{1,2},{2,1},{3,4},{4,3},{5,6},{6,5},{9,10},{10,9},{11,12},{12,11},... | collective-permute-start | bytes 3244040 | tf_op jit(solution)/shard_map/ppermute | solution.py:425
  108.9 1.1 copy-start.2
  110.0 2.6 %collective-permute-start.6 = (f32[8,3,80,128]{3,2,1,0:T(8,128)S(1)}, f32[8,3,80,128]{3,2,1,0:T(8,128)S(1)}, u32[]{:S(2)}, u32[]{:S(2)}) collective-permute-start(f32[8,3,80,128]{3,2,1,0:T(8,128)S(1)} %get-tuple-element.24), channel_id=1, source_target_pairs={{0,1},{1,0},{2,3},{3,2},{4,5},{5,4},{6,7},{7,6},{8,9},{9,8},{10,11... | collective-permute-start | bytes 2949128 | tf_op jit(solution)/shard_map/ppermute | solution.py:422
  110.4 15.4 %collective-permute-start.7 = (f32[8,3,80,128]{3,2,1,0:T(8,128)S(1)}, f32[8,3,80,128]{3,2,1,0:T(8,128)S(1)}, u32[]{:S(2)}, u32[]{:S(2)}) collective-permute-start(f32[8,3,80,128]{3,2,1,0:T(8,128)S(1)} %get-tuple-element.25), channel_id=1, source_target_pairs={{1,2},{2,1},{3,4},{4,3},{5,6},{6,5},{9,10},{10,9},{11,12},{12,11},... | collective-permute-start | bytes 2949128 | tf_op jit(solution)/shard_map/ppermute | solution.py:425
  125.8 26.9 %copy-start = (f32[3,12,112,128]{3,2,1,0:T(8,128)S(1)}, f32[3,12,112,128]{3,2,1,0:T(8,128)}, u32[]{:S(2)}) copy-start(f32[3,12,112,128]{3,2,1,0:T(8,128)} %get-tuple-element.17.coef_ref) | copy-start | bytes 6193156
  125.8 26.9 %copy-start.3 = (f32[8,8]{1,0:T(8,128)S(1)}, f32[8,8]{1,0:T(8,128)}, u32[]{:S(2)}) copy-start(f32[8,8]{1,0:T(8,128)} %constant.33.clone.table_ref) | copy-start | bytes 772
  138.1 2.5 %collective-permute-start.8 = (f32[8,3,72,128]{3,2,1,0:T(8,128)S(1)}, f32[8,3,72,128]{3,2,1,0:T(8,128)S(1)}, u32[]{:S(2)}, u32[]{:S(2)}) collective-permute-start(f32[8,3,72,128]{3,2,1,0:T(8,128)S(1)} %get-tuple-element.27), channel_id=1, source_target_pairs={{0,1},{1,0},{2,3},{3,2},{4,5},{5,4},{6,7},{7,6},{8,9},{9,8},{10,11... | collective-permute-start | bytes 2654216 | tf_op jit(solution)/shard_map/ppermute | solution.py:422
  138.3 14.3 %collective-permute-start.9 = (f32[8,3,72,128]{3,2,1,0:T(8,128)S(1)}, f32[8,3,72,128]{3,2,1,0:T(8,128)S(1)}, u32[]{:S(2)}, u32[]{:S(2)}) collective-permute-start(f32[8,3,72,128]{3,2,1,0:T(8,128)S(1)} %get-tuple-element.28), channel_id=1, source_target_pairs={{1,2},{2,1},{3,4},{4,3},{5,6},{6,5},{9,10},{10,9},{11,12},{12,11},... | collective-permute-start | bytes 2654216 | tf_op jit(solution)/shard_map/ppermute | solution.py:425

commit v2 on v0

v2 whole, which is shorter than its diff:
```python
import functools
import math

import jax
import jax.numpy as jnp
import numpy as np
from jax import lax
from jax.experimental import pallas as pl
from jax.experimental.pallas import tpu as pltpu
from jax.sharding import PartitionSpec as P

SWEEPS = 12
DEPTH = 3
YHALO = 16
PAD = 8
GROUPS = 2
LIMIT = 24 * 1024 * 1024
COST = 5_000_000

cheb_centre = 1.0
cheb_half = 0.7

VMEM = pl.BlockSpec(memory_space=pltpu.VMEM)
SMEM = pl.BlockSpec(memory_space=pltpu.SMEM)


def omegas():
    return [
        1.0
        / (cheb_centre + cheb_half * math.cos(math.pi * (2 * turn + 1) / (2 * SWEEPS)))
        for turn in range(SWEEPS)
    ]


def mode_terms(total):
    time = np.arange(total)
    table = np.zeros((total, total))
    table[0] = 1.0
    table[1] = np.where(time % 2 == 0, 1.0, -1.0)
    for mode in range(1, total // 2):
        angle = 2.0 * np.pi * (mode * time % total) / total
        table[2 * mode] = np.cos(angle)
        table[2 * mode + 1] = -np.sin(angle)
    table[np.abs(table) < 1e-9] = 0.0
    return table


def weighted(values, weights):
    groups = {}
    for value, weight in zip(values, weights):
        size = round(abs(float(weight)), 12)
        if size == 0.0:
            continue
        sign = 1 if weight > 0 else -1
        groups.setdefault(size, []).append((sign, value))
    total = None
    for size, members in groups.items():
        sign, part = members[0]
        lead = sign
        for sign, value in members[1:]:
            part = part + value if sign == lead else part - value
        factor = lead * size
        if factor != 1.0:
            part = part * factor
        total = part if total is None else total + part
    return total


def spectra(values):
    total = len(values)
    half = total // 2
    table = mode_terms(total)
    even = [values[0]] + [values[n] + values[total - n] for n in range(1, half)] + [values[half]]
    odd = [values[n] - values[total - n] for n in range(1, half)]
    fields = [weighted(even, table[0][: half + 1]), weighted(even, table[1][: half + 1])]
    for mode in range(1, half):
        fields.append(weighted(even, table[2 * mode][: half + 1]))
        fields.append(weighted(odd, table[2 * mode + 1][1:half]))
    return fields


def near_sum(w_ref, lead, coef_ref, plane, row, shift=0):
    lanes = w_ref.shape[-1]
    at = pl.ds(row, 8)
    below = pl.ds(row - 1, 8)
    above = pl.ds(row + 1, 8)
    mine = plane - shift
    core = w_ref[lead, mine, at, :]
    face = coef_ref[2, plane, at, :]
    total = coef_ref[0, plane, at, :] * w_ref[lead, mine - 1, at, :]
    total = total + coef_ref[0, plane + 1, at, :] * w_ref[lead, mine + 1, at, :]
    total = total + coef_ref[1, plane, at, :] * w_ref[lead, mine, below, :]
    total = total + coef_ref[1, plane, above, :] * w_ref[lead, mine, above, :]
    total = total + face * pltpu.roll(core, 1, 1)
    total = total + pltpu.roll(face * core, lanes - 1, 1)
    return core, total


def sweep(source, target, coef_ref, w0_ref, inv_ref, pair, omega, planes, chunks):
    first, count = planes

    def two(turn, _):
        for side in range(2):
            plane = first + 2 * turn + side
            for chunk in chunks:
                row = PAD + 8 * chunk
                at = pl.ds(8 * chunk, 8)
                core_a, sum_a = near_sum(source, 0, coef_ref, plane, row)
                core_b, sum_b = near_sum(source, 1, coef_ref, plane, row)
                inv_a = inv_ref[3 * pair, plane - 1, at, :]
                inv_b = inv_ref[3 * pair + 1, plane - 1, at, :]
                cross = inv_ref[3 * pair + 2, plane - 1, at, :]
                term_a = w0_ref[2 * pair, plane - 1, at, :] + (inv_a * sum_a - cross * sum_b)
                term_b = w0_ref[2 * pair + 1, plane - 1, at, :] + (inv_b * sum_b + cross * sum_a)
                target[0, plane, pl.ds(row, 8), :] = (1.0 - omega) * core_a + omega * term_a
                target[1, plane, pl.ds(row, 8), :] = (1.0 - omega) * core_b + omega * term_b
        return 0

    lax.fori_loop(0, count // 2, two, 0)


def chunks_of(rows, halo):
    first = (YHALO - halo) // 8
    return range(max(first, 0), min(rows // 8 - first, rows // 8))


def sweeps_on(buffers, coef_ref, w0_ref, inv_ref, pair, done, block, rows):
    own = DEPTH + 1
    for step in range(DEPTH):
        reach = DEPTH - 1 - step
        sweep(
            buffers[step % 2],
            buffers[(step + 1) % 2],
            coef_ref,
            w0_ref,
            inv_ref,
            pair,
            omegas()[done + step],
            (own - reach, block + 2 * reach),
            chunks_of(rows, SWEEPS - 1 - done - step),
        )
    return buffers[DEPTH % 2]


def send_out(result, pair, parity, own_ref, on_ref, off_ref, block, own_window, window):
    own = DEPTH + 1
    first_on = own + jnp.where(parity == 0, block - DEPTH, 0)
    first_off = own + jnp.where(parity == 0, 0, block - DEPTH)
    own_at = pl.ds(PAD + own_window[0], own_window[1])
    at = pl.ds(PAD + window[0], window[1])
    for which in range(2):
        for plane in range(DEPTH):
            off_ref[2 * pair + which, plane] = result[which, first_off + plane, at, :]
            on_ref[2 * pair + which, plane] = result[which, first_on + plane, at, :]
        for plane in range(block):
            own_ref[2 * pair + which, plane] = result[which, own + plane, own_at, :]


def load_in(buffer_a, pair, parity, own_ref, on_ref, off_ref, block, own_window, window):
    own = DEPTH + 1
    own_at = pl.ds(PAD + own_window[0], own_window[1])
    at = pl.ds(PAD + window[0], window[1])
    first_on = jnp.where(parity == 0, own + block, 1)
    first_off = jnp.where(parity == 0, 1, own + block)
    for which in range(2):
        for plane in range(block):
            buffer_a[which, own + plane, own_at, :] = own_ref[2 * pair + which, plane]
        for plane in range(DEPTH):
            buffer_a[which, first_on + plane, at, :] = on_ref[2 * pair + which, plane]
            buffer_a[which, first_off + plane, at, :] = off_ref[2 * pair + which, plane]


def clear_edges(refs, rows, depth):
    blank = jnp.zeros((PAD + depth, refs[0].shape[-1]), jnp.float32)

    def clear(plane, _):
        for ref in refs:
            for lead in range(ref.shape[0]):
                ref[lead, plane, pl.ds(0, PAD + depth), :] = blank
                ref[lead, plane, pl.ds(rows + PAD - depth, PAD + depth), :] = blank
        return 0

    lax.fori_loop(0, refs[0].shape[1], clear, 0)


def pack_kernel(chunk, weights_ref, state_ref, out_ref):
    step = pl.program_id(0)
    pieces, _, block, rows, lanes = out_ref.shape
    length = state_ref.shape[2]
    for plane in range(block):
        for piece in range(pieces):
            low = piece * chunk - YHALO
            first, last = max(low, 0), min(low + rows, length)
            if first > low:
                out_ref[piece, 0, plane, pl.ds(0, first - low), :] = jnp.zeros(
                    (first - low, lanes), jnp.float32
                )
            if last < low + rows:
                out_ref[piece, 0, plane, pl.ds(last - low, low + rows - last), :] = jnp.zeros(
                    (low + rows - last, lanes), jnp.float32
                )
            out_ref[piece, 0, plane, pl.ds(first - low, last - first), :] = state_ref[
                0, plane, pl.ds(first, last - first), :
            ]
    for piece in range(pieces):
        out_ref[piece, 0, 0, pl.ds(0, 1), :] = jnp.full((1, lanes), weights_ref[step], jnp.float32)


def finish_kernel(weights_ref, state_ref, back_ref, out_ref):
    step = pl.program_id(0)
    pieces, _, block, chunk, lanes = back_ref.shape
    weight = jnp.full((8, lanes), weights_ref[step], jnp.float32)
    scale = (1.0 / weight)[:1]
    for plane in range(block):
        for piece in range(pieces):
            at = pl.ds(piece * chunk, chunk)
            out_ref[0, plane, at, :] = state_ref[0, plane, at, :] + back_ref[piece, 0, plane] * scale


def residual_starts(wide, base, planes, state_own, field_of, coef_ref, diag_ref, inv_ref, w0_refs):
    total = wide.shape[0]
    rows = diag_ref.shape[1]
    half = total // 2
    first, count = planes

    def one(turn, _):
        plane = first + turn
        for chunk in range(rows // 8):
            row = PAD + 8 * chunk
            at = pl.ds(8 * chunk, 8)
            around = diag_ref[plane - 1, at, :]
            values = []
            for lead in range(total):
                core, near = near_sum(wide, lead, coef_ref, plane, row, base)
                if lead == 0:
                    prior = field_of(plane, row)
                else:
                    prior = wide[lead - 1, plane - base, pl.ds(row, 8), :]
                value = prior - (around * core - near) - core * core * core
                values.append(value * state_own[lead, 0, pl.ds(0, 1), :])
            fields = spectra(values)
            for pair in range(half):
                spec_a, spec_b = fields[2 * pair], fields[2 * pair + 1]
                inv_a = inv_ref[3 * pair, plane - 1, at, :]
                inv_b = inv_ref[3 * pair + 1, plane - 1, at, :]
                cross = inv_ref[3 * pair + 2, plane - 1, at, :]
                w_a = inv_a * spec_a - cross * spec_b
                w_b = inv_b * spec_b + cross * spec_a
                put(w0_refs, 2 * pair, plane - 1, at, w_a)
                put(w0_refs, 2 * pair + 1, plane - 1, at, w_b)
        return 0

    lax.fori_loop(0, count, one, 0)


def put(refs, lead, plane, at, value):
    per = refs[0].shape[0]
    refs[lead // per][lead % per, plane, at, :] = value


def early_kernel(
    parity_ref,
    shift_real_ref,
    shift_imag_ref,
    state_own,
    state_on,
    fixed_own,
    fixed_on,
    fixed_off,
    coef_ref,
    diag_ref,
    inv_ref,
    w0_ref,
    wide,
    fixed,
):
    total, block, rows, lanes = state_own.shape
    half = total // 2
    own = DEPTH + 1
    planes = block + 2 * own
    parity = parity_ref[0]
    first_on = jnp.where(parity == 0, own + block, 0)
    first_off = jnp.where(parity == 0, 0, own + block)
    base = jnp.where(parity == 0, own, 0)
    clear_edges((fixed, coef_ref), rows, 0)
    clear_edges((wide,), rows, 0)
    body = pl.ds(PAD, rows)

    def place(plane, _):
        for lead in range(total):
            wide[lead, own - base + plane, body, :] = state_own[lead, plane]
            wide[lead, first_on - base + plane, body, :] = state_on[lead, plane]
        for lead in range(2):
            fixed[lead, own + plane, body, :] = fixed_own[lead, plane]
            fixed[lead, first_on + plane, body, :] = fixed_on[lead, plane]
            fixed[lead, first_off + plane, body, :] = fixed_off[lead, plane]
        return 0

    lax.fori_loop(0, block, place, 0)
    lane = lax.broadcasted_iota(jnp.int32, (8, lanes), 1)

    def faces(plane, _):
        for chunk in range(rows // 8):
            row = PAD + 8 * chunk
            at = pl.ds(row, 8)
            kappa = fixed[1, plane, at, :]
            coef_ref[0, plane, at, :] = 0.5 * (fixed[1, plane - 1, at, :] + kappa)
            coef_ref[1, plane, at, :] = 0.5 * (fixed[1, plane, pl.ds(row - 1, 8), :] + kappa)
            near = 0.5 * (pltpu.roll(kappa, 1, 1) + kappa)
            coef_ref[2, plane, at, :] = jnp.where(lane == 0, 0.0, near)
        return 0

    lax.fori_loop(1, planes, faces, 0)
    reals = [shift_real_ref[mode] for mode in range(half + 1)]
    imags = [shift_imag_ref[mode] for mode in range(half)]

    def inverses(plane, _):
        for chunk in range(rows // 8):
            row = PAD + 8 * chunk
            at = pl.ds(row, 8)
            out = pl.ds(8 * chunk, 8)
            kappa = fixed[1, plane, at, :]
            low = 0.5 * (kappa + jnp.where(lane == 0, 0.0, pltpu.roll(kappa, 1, 1)))
            high = 0.5 * (kappa + jnp.where(lane == lanes - 1, 0.0, pltpu.roll(kappa, lanes - 1, 1)))
            around = coef_ref[0, plane, at, :] + coef_ref[0, plane + 1, at, :]
            around = around + coef_ref[1, plane, at, :]
            around = around + coef_ref[1, plane, pl.ds(row + 1, 8), :]
            around = around + low + high
            diag_ref[plane - 1, out, :] = around
            inside = kappa > 0.0
            zero = jnp.zeros_like(kappa)
            inv_ref[0, plane - 1, out, :] = jnp.where(inside, 1.0 / (reals[0] + around), 0.0)
            inv_ref[1, plane - 1, out, :] = jnp.where(inside, 1.0 / (reals[half] + around), 0.0)
            inv_ref[2, plane - 1, out, :] = zero
            for mode in range(1, half):
                denom = reals[mode] + around
                scale = jnp.where(inside, 1.0 / (denom * denom + imags[mode] * imags[mode]), 0.0)
                value = denom * scale
                inv_ref[3 * mode, plane - 1, out, :] = value
                inv_ref[3 * mode + 1, plane - 1, out, :] = value
                inv_ref[3 * mode + 2, plane - 1, out, :] = -imags[mode] * scale
        return 0

    lax.fori_loop(1, planes - 1, inverses, 0)

    def field_of(plane, row):
        return fixed[0, plane, pl.ds(row, 8), :]

    count = block + own - 2
    first = jnp.where(parity == 0, planes - 1 - count, 1)
    residual_starts(
        wide, base, (first, count), state_own, field_of, coef_ref, diag_ref, inv_ref, (w0_ref,)
    )


def late_kernel(
    parity_ref,
    state_own,
    state_off,
    fixed_own,
    fixed_off,
    coef_ref,
    diag_ref,
    inv_ref,
    w0_in,
    *rest,
):
    w0_refs, wide, field = rest[:-2], rest[-2], rest[-1]
    total, block, rows, lanes = state_own.shape
    own = DEPTH + 1
    planes = block + 2 * own
    parity = parity_ref[0]
    base = jnp.where(parity == 0, 0, planes - own - 2)
    first_off = jnp.where(parity == 0, 0, 2)
    first_own = jnp.where(parity == 0, own, 0)
    from_own = jnp.where(parity == 0, 0, block - 2)
    clear_edges((wide,), rows, 0)
    body = pl.ds(PAD, rows)

    def place_off(plane, _):
        for lead in range(total):
            wide[lead, first_off + plane, body, :] = state_off[lead, plane]
        field[first_off + plane, body, :] = fixed_off[0, plane]
        return 0

    def place_own(plane, _):
        for lead in range(total):
            wide[lead, first_own + plane, body, :] = state_own[lead, from_own + plane]
        field[first_own + plane, body, :] = fixed_own[0, from_own + plane]
        return 0

    lax.fori_loop(0, block, place_off, 0)
    lax.fori_loop(0, 2, place_own, 0)
    count = block + own - 2
    first = jnp.where(parity == 0, planes - 1 - count, 1)

    def copy(turn, _):
        for lead in range(total):
            put(w0_refs, lead, first - 1 + turn, slice(None), w0_in[lead, first - 1 + turn])
        return 0

    lax.fori_loop(0, count, copy, 0)

    def field_of(plane, row):
        return field[plane - base, pl.ds(row, 8), :]

    residual_starts(
        wide, base, (base + 1, own), state_own, field_of, coef_ref, diag_ref, inv_ref, w0_refs
    )


def first_kernel(
    low_pair,
    own_window,
    window,
    parity_ref,
    coef_ref,
    w0_ref,
    inv_ref,
    own_ref,
    on_ref,
    off_ref,
    buffer_a,
    buffer_b,
):
    parity = parity_ref[0]
    block = own_ref.shape[1]
    rows = w0_ref.shape[2]
    clear_edges((buffer_a, buffer_b), rows, 0)
    group_inv = inv_ref.at[pl.ds(3 * low_pair, 3 * (w0_ref.shape[0] // 2))]

    def one(pair, _):
        def copy(plane, _):
            for which in range(2):
                buffer_a[which, plane + 1, pl.ds(PAD, rows), :] = w0_ref[2 * pair + which, plane]
            return 0

        lax.fori_loop(0, w0_ref.shape[1], copy, 0)
        result = sweeps_on((buffer_a, buffer_b), coef_ref, w0_ref, group_inv, pair, 0, block, rows)
        send_out(result, pair, parity, own_ref, on_ref, off_ref, block, own_window, window)
        return 0

    lax.fori_loop(0, w0_ref.shape[0] // 2, one, 0)


def middle_kernel(
    low_pair,
    done,
    windows,
    next_windows,
    parity_ref,
    coef_ref,
    own_in,
    on_in,
    off_in,
    w0_ref,
    inv_ref,
    own_ref,
    on_ref,
    off_ref,
    buffer_a,
    buffer_b,
):
    parity = parity_ref[0]
    block = own_in.shape[1]
    rows = w0_ref.shape[2]
    clear_edges((buffer_a, buffer_b), rows, 16)
    group_inv = inv_ref.at[pl.ds(3 * low_pair, 3 * (w0_ref.shape[0] // 2))]

    def one(pair, _):
        load_in(buffer_a, pair, parity, own_in, on_in, off_in, block, *windows)
        result = sweeps_on((buffer_a, buffer_b), coef_ref, w0_ref, group_inv, pair, done, block, rows)
        send_out(result, pair, parity, own_ref, on_ref, off_ref, block, *next_windows)
        return 0

    lax.fori_loop(0, w0_ref.shape[0] // 2, one, 0)


def last_kernel(low_pair, done, windows, parity_ref, coef_ref, own_in, on_in, off_in, w0_ref, inv_ref, *rest):
    out_ref, buffer_a, buffer_b = rest[-3:]
    parity = parity_ref[0]
    block = own_in.shape[1]
    rows = w0_ref.shape[2]
    total, chunk_rows = out_ref.shape[0], out_ref.shape[2]
    pairs = w0_ref.shape[0] // 2
    own = DEPTH + 1
    clear_edges((buffer_a, buffer_b), rows, 16)
    group_inv = inv_ref.at[pl.ds(3 * low_pair, 3 * pairs)]
    table = mode_terms(total).T / total
    table[:, 2:] *= 2.0
    half = total // 2
    for pair in range(pairs):
        mode = low_pair + pair
        load_in(buffer_a, pair, parity, own_in, on_in, off_in, block, *windows)
        result = sweeps_on((buffer_a, buffer_b), coef_ref, w0_ref, group_inv, pair, done, block, rows)
        before = None
        if pair > 0:
            before = out_ref
        elif len(rest) == 4:
            before = rest[0]

        def one(plane, _):
            for chunk in range(chunk_rows // 8):
                at = pl.ds(8 * chunk, 8)
                row = pl.ds(PAD + YHALO + 8 * chunk, 8)
                w_a = result[0, own + plane, row, :]
                w_b = result[1, own + plane, row, :]
                for lead in range(total):
                    value = weighted((w_a, w_b), table[lead, 2 * mode : 2 * mode + 2])
                    if before is not None:
                        value = value + before[lead, plane, at, :]
                    out_ref[lead, plane, at, :] = value
            return 0

        lax.fori_loop(0, block, one, 0)


def shards(state, start_field, diffusivity, time_weights, shift_real, shift_imag):
    steps, block, length, lanes = state.shape
    pieces = lax.axis_size("tm")
    slabs = lax.axis_size("gx")
    total = steps * pieces
    pairs = total // 2
    per = pairs // GROUPS
    chunk = length // pieces
    rows = chunk + 2 * YHALO
    own = DEPTH + 1
    planes = block + 2 * own
    padded = rows + 2 * PAD
    f32 = jnp.float32
    device = lax.axis_index("tm")
    parity = (lax.axis_index("gx") % 2).astype(jnp.int32).reshape((1,))
    on_pairs = [(i, i ^ 1) for i in range(slabs)]
    off_pairs = []
    for i in range(1, slabs - 1, 2):
        off_pairs += [(i, i + 1), (i + 1, i)]

    def shape(*dims):
        return jax.ShapeDtypeStruct(dims, f32)

    def swap_on(value, name):
        with jax.named_scope(f"{name}_on"):
            return lax.ppermute(value, "gx", on_pairs)

    def swap_off(value, name):
        with jax.named_scope(f"{name}_off"):
            return lax.ppermute(value, "gx", off_pairs)

    def call(kernel, name, inputs, scalars, outs, scratch, flops):
        return pl.pallas_call(
            kernel,
            in_specs=[SMEM] * scalars + [VMEM] * (len(inputs) - scalars),
            out_specs=[VMEM] * len(outs),
            out_shape=outs,
            scratch_shapes=[pltpu.VMEM(dims, f32) for dims in scratch],
            compiler_params=pltpu.CompilerParams(vmem_limit_bytes=LIMIT),
            cost_estimate=pl.CostEstimate(flops=flops, bytes_accessed=flops, transcendentals=0),
            name=name,
        )(*inputs)

    fixed = jnp.pad(jnp.stack([start_field, diffusivity]), ((0, 0), (0, 0), (YHALO, YHALO), (0, 0)))
    fixed = lax.dynamic_slice_in_dim(fixed, device * chunk, rows, axis=2)
    fixed_off = swap_off(fixed, "fixed")
    fixed_on = swap_on(fixed, "fixed")

    step_spec = pl.BlockSpec((1, block, length, lanes), lambda i: (i, 0, 0, 0))
    packed = pl.pallas_call(
        functools.partial(pack_kernel, chunk),
        grid=(steps,),
        in_specs=[SMEM, step_spec],
        out_specs=pl.BlockSpec((pieces, 1, block, rows, lanes), lambda i: (0, i, 0, 0, 0)),
        out_shape=shape(pieces, steps, block, rows, lanes),
        name="pack",
    )(time_weights, state)
    with jax.named_scope("mix"):
        mixed = lax.all_to_all(packed, "tm", split_axis=0, concat_axis=0, tiled=True)
    mixed = mixed.reshape((total, block, rows, lanes))
    mixed_off = swap_off(mixed, "state")
    mixed_on = swap_on(mixed, "state")

    def window_of(halo):
        low = (YHALO - halo) // 4 * 4
        return low, rows - 2 * low

    windows = []
    for phase in range(1, SWEEPS // DEPTH):
        left = SWEEPS - DEPTH * phase
        windows.append((window_of(left), window_of(left - 1)))

    coefs, diag, inverse, w0 = call(
        early_kernel,
        "early",
        (parity, shift_real, shift_imag, mixed, mixed_on, fixed, fixed_on, fixed_off),
        3,
        [
            shape(3, planes, padded, lanes),
            shape(planes - 2, rows, lanes),
            shape(3 * pairs, planes - 2, rows, lanes),
            shape(total, planes - 2, rows, lanes),
        ],
        [(total, planes - own, padded, lanes), (2, planes, padded, lanes)],
        COST,
    )
    starts = call(
        late_kernel,
        "late",
        (parity, mixed, mixed_off, fixed, fixed_off, coefs, diag, inverse, w0),
        1,
        [shape(2 * per, planes - 2, rows, lanes)] * GROUPS,
        [(total, own + 2, padded, lanes), (own + 2, padded, lanes)],
        COST,
    )
    buffers = [(2, planes, padded, lanes)] * 2

    def sent(pair_windows):
        own_window, window = pair_windows
        return [
            shape(2 * per, block, own_window[1], lanes),
            shape(2 * per, DEPTH, window[1], lanes),
            shape(2 * per, DEPTH, window[1], lanes),
        ]

    moving = []
    for group in range(GROUPS):
        own_w, on_w, off_w = call(
            functools.partial(first_kernel, per * group, *windows[0]),
            f"first{group}",
            (parity, coefs, starts[group], inverse),
            1,
            sent(windows[0]),
            buffers,
            COST,
        )
        moving.append((own_w, swap_on(on_w, f"a{group}"), swap_off(off_w, f"a{group}")))
    last = SWEEPS // DEPTH - 1
    for phase in range(1, last):
        for group in range(GROUPS):
            own_w, on_w, off_w = call(
                functools.partial(
                    middle_kernel, per * group, DEPTH * phase, windows[phase - 1], windows[phase]
                ),
                f"middle{phase}{group}",
                (parity, coefs, *moving[group], starts[group], inverse),
                1,
                sent(windows[phase]),
                buffers,
                COST,
            )
            name = "abcdefgh"[phase] + str(group)
            moving[group] = (own_w, swap_on(on_w, name), swap_off(off_w, name))
    delta = ()
    for group in range(GROUPS):
        delta = call(
            functools.partial(last_kernel, per * group, DEPTH * last, windows[last - 1]),
            f"last{group}",
            (parity, coefs, *moving[group], starts[group], inverse, *delta),
            1,
            [shape(total, block, chunk, lanes)],
            buffers,
            COST,
        )
    with jax.named_scope("back"):
        back = lax.all_to_all(
            delta[0].reshape((pieces, steps, block, chunk, lanes)),
            "tm",
            split_axis=0,
            concat_axis=0,
            tiled=True,
        )
    return pl.pallas_call(
        finish_kernel,
        grid=(steps,),
        in_specs=[
            SMEM,
            step_spec,
            pl.BlockSpec((pieces, 1, block, chunk, lanes), lambda i: (0, i, 0, 0, 0)),
        ],
        out_specs=step_spec,
        out_shape=shape(steps, block, length, lanes),
        name="finish",
    )(time_weights, state, back)


def solution(mesh):
    in_specs = (
        P("tm", "gx", None, None),
        P("gx", None, None),
        P("gx", None, None),
        P("tm"),
        P(),
        P(),
    )
    out_specs = P("tm", "gx", None, None)
    return jax.shard_map(shards, mesh=mesh, in_specs=in_specs, out_specs=out_specs, check_vma=False)
```

time: 404 us -> 137 us (0.34)
  waiting for transfers between devices: 152 us -> 23.5 us
  local copies, waits for them, and re-layouts: 90 us -> 0.01 us
  other arithmetic: 72.5 us -> 1.05 us
  starting transfers between devices: 76.5 us -> 24.4 us
  Pallas kernels: 0 us -> 45.4 us
  blocking collectives: 0 us -> 41.5 us
  matrix products: 6.04 us -> 0 us
    all_to_all x4 -> x0, waiting for transfers between devices: 90.9 us -> none  [the longest x1 24.6 us: shards(): lax.all_to_all(field, 'tm', split_axis=3, concat_axis=0, tiled=True)]
    slice x41 -> x0, local copies, waits for them, and re-layouts: 55.2 us -> none  [the longest x26 38.9 us: along(): lax.slice_in_dim(core, 0, length - 1, axis=axis)]
    pallas_call x0 -> x12, Pallas kernels: none -> 45.4 us  [the longest x10 40.8 us: call(): pl.pallas_call(kernel, in_specs=[SMEM] * scalars + [VMEM] * (len(inputs)...]
    sub x13 -> x0, other arithmetic: 42.2 us -> none  [the longest x12 40.3 us: operate(): return diag_sum * core - total]
    all_to_all x0 -> x2, blocking collectives: none -> 41.5 us  [the longest x1 23.7 us: shards(): lax.all_to_all(packed, 'tm', split_axis=0, concat_axis=0, tiled=True)]
    ppermute x27 -> x16, waiting for transfers between devices: 61.4 us -> 23.5 us  [the longest x8 23.5 us: swap_off(): return lax.ppermute(value, 'gx', off_pairs)]
    ppermute x27 -> x16, starting transfers between devices: 61.6 us -> 24.4 us  [the longest x8 20.9 us: swap_off(): return lax.ppermute(value, 'gx', off_pairs)]
    add x27 -> x0, other arithmetic: 19.9 us -> none  [the longest x12 9.55 us: sweep(): answer_real + omega * (misfit_real * inverse_real - misfit_imag * inverse...]
  transfers between devices with their start and end apart: 31 -> 16, of which waited for: 28 -> 5; matrix products, arithmetic and copies ran while one was open for 16% -> 1% of each run, Pallas kernels for 0% -> 22%
where the time goes in v2:
time: 137 us; the launch traced here: 136 us
  Pallas kernels  45.4 us (33%)
  blocking collectives  41.5 us (30%)
  starting transfers between devices  24.4 us (18%)
  waiting for transfers between devices  23.5 us (17%)
    pallas_call x10, Pallas kernels, call(): pl.pallas_call(kernel, in_specs=[SMEM] * scalars + [VMEM] * (len(inputs)...  40.8 us
    all_to_all x1, blocking collectives, shards(): lax.all_to_all(packed, 'tm', split_axis=0, concat_axis=0, tiled=True)  23.7 us
    ppermute x8, waiting for transfers between devices, swap_off(): return lax.ppermute(value, 'gx', off_pairs)  23.5 us
    ppermute x8, starting transfers between devices, swap_off(): return lax.ppermute(value, 'gx', off_pairs)  20.9 us
    all_to_all x1, blocking collectives, shards(): lax.all_to_all(delta[0].reshape((pieces, steps, block, chunk, lanes)), 't...  17.8 us
    ppermute x8, starting transfers between devices, swap_on(): return lax.ppermute(value, 'gx', on_pairs)  3.52 us
  transfers between devices with their start and end apart: 16, of which 5 were waited for; matrix products, arithmetic and copies ran while one was open for 1% of the time, Pallas kernels for 22%

profile of v2, /device:TPU:16, one launch (start us, length us, event | category | flops | bytes accessed | tf_op | source)
XLA Modules:
  0.0 136.2 jit_solution(7898123311135584035)
XLA Ops:
  0.0 2.3 %pack.1 = f32[4,2,4,96,128]{4,3,2,1,0:T(8,128)} custom-call(f32[2]{0:T(128)} %weights_ref.3, f32[2,4,256,128]{3,2,1,0:T(8,128)} %state_ref.3), custom_call_target="tpu_custom_call" | custom-call | tf_op jit(solution)/shard_map/pack/pallas_call | solution.py:567
  2.3 23.7 %all_to_all.10 = f32[4,2,4,96,128]{4,3,2,1,0:T(8,128)S(1)} all-to-all(f32[4,2,4,96,128]{4,3,2,1,0:T(8,128)} %pack.1), channel_id=1, replica_groups=mesh['tm'=4,'gx'=8] {'tm'}, dimensions={0} | all-to-all | bytes 3145728 | tf_op jit(solution)/shard_map/mix/all_to_all | solution.py:576
  26.0 2.5 %collective-permute-start.3 = (f32[8,4,96,128]{3,2,1,0:T(8,128)S(1)}, f32[8,4,96,128]{3,2,1,0:T(8,128)S(1)}, u32[]{:S(2)}, u32[]{:S(2)}) collective-permute-start(f32[8,4,96,128]{3,2,1,0:T(8,128)S(1)} %bitcast.6), channel_id=1, source_target_pairs={{1,2},{2,1},{3,4},{4,3},{5,6},{6,5},{9,10},{10,9},{11,12},{12,11},... | collective-permute-start | bytes 4718600 | tf_op jit(solution)/shard_map/state_off/ppermute | solution.py:547
  28.4 1.1 fusion.1.fixed_own
  29.5 3.1 %collective-permute-start.2 = (f32[2,4,96,128]{3,2,1,0:T(8,128)S(1)}, f32[2,4,96,128]{3,2,1,0:T(8,128)}, u32[]{:S(2)}, u32[]{:S(2)}) collective-permute-start(f32[2,4,96,128]{3,2,1,0:T(8,128)S(1)} %fusion.1.fixed_own), channel_id=1, source_target_pairs={{1,2},{2,1},{3,4},{4,3},{5,6},{6,5},{9,10},{10,9},{11,12},{12,11},... | collective-permute-start | bytes 1179656 | tf_op jit(solution)/shard_map/fixed_off/ppermute | solution.py:547
  32.6 0.6 collective-permute-start.1
  33.2 18.8 %collective-permute-done.2.fixed_off = f32[2,4,96,128]{3,2,1,0:T(8,128)} collective-permute-done((f32[2,4,96,128]{3,2,1,0:T(8,128)S(1)}, f32[2,4,96,128]{3,2,1,0:T(8,128)}, u32[]{:S(2)}, u32[]{:S(2)}) %collective-permute-start.2) | collective-permute-done | bytes 393248 | tf_op jit(solution)/shard_map/fixed_off/ppermute | solution.py:547
  52.0 7.0 %early.1 = (f32[3,12,112,128]{3,2,1,0:T(8,128)S(1)}, f32[10,96,128]{2,1,0:T(8,128)S(1)}, f32[12,10,96,128]{3,2,1,0:T(8,128)S(1)}, f32[8,10,96,128]{3,2,1,0:T(8,128)S(1)}) custom-call(s32[1]{0:T(128)} %bitcast.parity_ref, f32[8]{0:T(128)S(1)} %copy-done, f32[8]{0:T(128)S(1)} %copy-done.1, f32[8,4,96,128]{3,2,1,0:T(8,128)S(1)} %bitcast.7, ...), custom_call_target="tpu_custom_call" | custom-call | flops 5000000 | bytes 5000000 | tf_op jit(solution)/shard_map/early/pallas_call | solution.py:550
  59.1 3.0 %late.1 = (f32[4,10,96,128]{3,2,1,0:T(8,128)S(1)}, f32[4,10,96,128]{3,2,1,0:T(8,128)S(1)}) custom-call(s32[1]{0:T(128)} %bitcast.parity_ref, f32[8,4,96,128]{3,2,1,0:T(8,128)S(1)} %bitcast.8, f32[8,4,96,128]{3,2,1,0:T(8,128)S(1)} %collective-permute-done.3.state_off, f32[2,4,96,128]{3,2,1,0:T(8,128)S(1)} %fusion.1.fixed_own, ...), custom_call_target="tpu_custom_call" | custom-call | flops 5000000 | bytes 5000000 | tf_op jit(solution)/shard_map/late/pallas_call | solution.py:550
  62.1 4.2 %first0.1 = (f32[4,4,88,128]{3,2,1,0:T(8,128)S(1)}, f32[4,3,80,128]{3,2,1,0:T(8,128)S(1)}, f32[4,3,80,128]{3,2,1,0:T(8,128)S(1)}) custom-call(s32[1]{0:T(128)} %bitcast.parity_ref, f32[3,12,112,128]{3,2,1,0:T(8,128)S(1)} %get-tuple-element.29.coef_ref, f32[4,10,96,128]{3,2,1,0:T(8,128)S(1)} %get-tuple-element.43.w0_ref, ...), custom_call_target="tpu_custom_call" | custom-call | flops 5000000 | bytes 5000000 | tf_op jit(solution)/shard_map/first0/pallas_call | solution.py:550
  66.3 0.6 collective-permute-start.10
  66.9 2.0 %collective-permute-start.11 = (f32[4,3,80,128]{3,2,1,0:T(8,128)S(1)}, f32[4,3,80,128]{3,2,1,0:T(8,128)S(1)}, u32[]{:S(2)}, u32[]{:S(2)}) collective-permute-start(f32[4,3,80,128]{3,2,1,0:T(8,128)S(1)} %get-tuple-element.46), channel_id=1, source_target_pairs={{1,2},{2,1},{3,4},{4,3},{5,6},{6,5},{9,10},{10,9},{11,12},{12,11},... | collective-permute-start | bytes 1474568 | tf_op jit(solution)/shard_map/a0_off/ppermute | solution.py:547
  68.9 4.2 %first1.1 = (f32[4,4,88,128]{3,2,1,0:T(8,128)S(1)}, f32[4,3,80,128]{3,2,1,0:T(8,128)S(1)}, f32[4,3,80,128]{3,2,1,0:T(8,128)S(1)}) custom-call(s32[1]{0:T(128)} %bitcast.parity_ref, f32[3,12,112,128]{3,2,1,0:T(8,128)S(1)} %get-tuple-element.29.coef_ref, f32[4,10,96,128]{3,2,1,0:T(8,128)S(1)} %get-tuple-element.33.w0_ref, ...), custom_call_target="tpu_custom_call" | custom-call | flops 5000000 | bytes 5000000 | tf_op jit(solution)/shard_map/first1/pallas_call | solution.py:550
  73.1 1.2 collective-permute-start.4
  74.3 2.5 %collective-permute-start.5 = (f32[4,3,80,128]{3,2,1,0:T(8,128)S(1)}, f32[4,3,80,128]{3,2,1,0:T(8,128)S(1)}, u32[]{:S(2)}, u32[]{:S(2)}) collective-permute-start(f32[4,3,80,128]{3,2,1,0:T(8,128)S(1)} %get-tuple-element.36), channel_id=1, source_target_pairs={{1,2},{2,1},{3,4},{4,3},{5,6},{6,5},{9,10},{10,9},{11,12},{12,11},... | collective-permute-start | bytes 1474568 | tf_op jit(solution)/shard_map/a1_off/ppermute | solution.py:547
  77.0 3.7 %middle10.1 = (f32[4,4,80,128]{3,2,1,0:T(8,128)S(1)}, f32[4,3,80,128]{3,2,1,0:T(8,128)S(1)}, f32[4,3,80,128]{3,2,1,0:T(8,128)S(1)}) custom-call(s32[1]{0:T(128)} %bitcast.parity_ref, f32[3,12,112,128]{3,2,1,0:T(8,128)S(1)} %get-tuple-element.29.coef_ref, f32[4,4,88,128]{3,2,1,0:T(8,128)S(1)} %get-tuple-element.44.own_in, ...), custom_call_target="tpu_custom_call" | custom-call | flops 5000000 | bytes 5000000 | tf_op jit(solution)/shard_map/middle10/pallas_call | solution.py:550
  80.9 2.7 %collective-permute-start.13 = (f32[4,3,80,128]{3,2,1,0:T(8,128)S(1)}, f32[4,3,80,128]{3,2,1,0:T(8,128)S(1)}, u32[]{:S(2)}, u32[]{:S(2)}) collective-permute-start(f32[4,3,80,128]{3,2,1,0:T(8,128)S(1)} %get-tuple-element.49), channel_id=1, source_target_pairs={{1,2},{2,1},{3,4},{4,3},{5,6},{6,5},{9,10},{10,9},{11,12},{12,11},... | collective-permute-start | bytes 1474568 | tf_op jit(solution)/shard_map/b0_off/ppermute | solution.py:547
  83.7 0.7 collective-permute-done.5.off_in
  84.4 3.7 %middle11.1 = (f32[4,4,80,128]{3,2,1,0:T(8,128)S(1)}, f32[4,3,80,128]{3,2,1,0:T(8,128)S(1)}, f32[4,3,80,128]{3,2,1,0:T(8,128)S(1)}) custom-call(s32[1]{0:T(128)} %bitcast.parity_ref, f32[3,12,112,128]{3,2,1,0:T(8,128)S(1)} %get-tuple-element.29.coef_ref, f32[4,4,88,128]{3,2,1,0:T(8,128)S(1)} %get-tuple-element.34.own_in, ...), custom_call_target="tpu_custom_call" | custom-call | flops 5000000 | bytes 5000000 | tf_op jit(solution)/shard_map/middle11/pallas_call | solution.py:550
  88.3 2.8 %collective-permute-start.7 = (f32[4,3,80,128]{3,2,1,0:T(8,128)S(1)}, f32[4,3,80,128]{3,2,1,0:T(8,128)S(1)}, u32[]{:S(2)}, u32[]{:S(2)}) collective-permute-start(f32[4,3,80,128]{3,2,1,0:T(8,128)S(1)} %get-tuple-element.39), channel_id=1, source_target_pairs={{1,2},{2,1},{3,4},{4,3},{5,6},{6,5},{9,10},{10,9},{11,12},{12,11},... | collective-permute-start | bytes 1474568 | tf_op jit(solution)/shard_map/b1_off/ppermute | solution.py:547
  91.2 3.7 %middle20.1 = (f32[4,4,72,128]{3,2,1,0:T(8,128)S(1)}, f32[4,3,72,128]{3,2,1,0:T(8,128)S(1)}, f32[4,3,72,128]{3,2,1,0:T(8,128)S(1)}) custom-call(s32[1]{0:T(128)} %bitcast.parity_ref, f32[3,12,112,128]{3,2,1,0:T(8,128)S(1)} %get-tuple-element.29.coef_ref, f32[4,4,80,128]{3,2,1,0:T(8,128)S(1)} %get-tuple-element.47.own_in, ...), custom_call_target="tpu_custom_call" | custom-call | flops 5000000 | bytes 5000000 | tf_op jit(solution)/shard_map/middle20/pallas_call | solution.py:550
  94.9 0.4 collective-permute-start.14
  95.3 2.8 %collective-permute-start.15 = (f32[4,3,72,128]{3,2,1,0:T(8,128)S(1)}, f32[4,3,72,128]{3,2,1,0:T(8,128)S(1)}, u32[]{:S(2)}, u32[]{:S(2)}) collective-permute-start(f32[4,3,72,128]{3,2,1,0:T(8,128)S(1)} %get-tuple-element.52), channel_id=1, source_target_pairs={{1,2},{2,1},{3,4},{4,3},{5,6},{6,5},{9,10},{10,9},{11,12},{12,11},... | collective-permute-start | bytes 1327112 | tf_op jit(solution)/shard_map/c0_off/ppermute | solution.py:547
  98.1 0.4 collective-permute-done.7.off_in
  98.5 3.7 %middle21.1 = (f32[4,4,72,128]{3,2,1,0:T(8,128)S(1)}, f32[4,3,72,128]{3,2,1,0:T(8,128)S(1)}, f32[4,3,72,128]{3,2,1,0:T(8,128)S(1)}) custom-call(s32[1]{0:T(128)} %bitcast.parity_ref, f32[3,12,112,128]{3,2,1,0:T(8,128)S(1)} %get-tuple-element.29.coef_ref, f32[4,4,80,128]{3,2,1,0:T(8,128)S(1)} %get-tuple-element.37.own_in, ...), custom_call_target="tpu_custom_call" | custom-call | flops 5000000 | bytes 5000000 | tf_op jit(solution)/shard_map/middle21/pallas_call | solution.py:550
  102.2 0.5 collective-permute-start.8
  102.6 2.5 %collective-permute-start.9 = (f32[4,3,72,128]{3,2,1,0:T(8,128)S(1)}, f32[4,3,72,128]{3,2,1,0:T(8,128)S(1)}, u32[]{:S(2)}, u32[]{:S(2)}) collective-permute-start(f32[4,3,72,128]{3,2,1,0:T(8,128)S(1)} %get-tuple-element.42), channel_id=1, source_target_pairs={{1,2},{2,1},{3,4},{4,3},{5,6},{6,5},{9,10},{10,9},{11,12},{12,11},... | collective-permute-start | bytes 1327112 | tf_op jit(solution)/shard_map/c1_off/ppermute | solution.py:547
  105.2 3.7 %last0.1.rest_0_ = f32[8,4,64,128]{3,2,1,0:T(8,128)S(1)} custom-call(s32[1]{0:T(128)} %bitcast.parity_ref, f32[3,12,112,128]{3,2,1,0:T(8,128)S(1)} %get-tuple-element.29.coef_ref, f32[4,4,72,128]{3,2,1,0:T(8,128)S(1)} %get-tuple-element.50.own_in, f32[4,3,72,128]{3,2,1,0:T(8,128)S(1)} %collective-permute-done.14.on_in, ...), custom_call_target="tpu_custom_call" | custom-call | flops 5000000 | bytes 5000000 | tf_op jit(solution)/shard_map/last0/pallas_call | solution.py:550
  109.0 3.3 %collective-permute-done.9.off_in = f32[4,3,72,128]{3,2,1,0:T(8,128)S(1)} collective-permute-done((f32[4,3,72,128]{3,2,1,0:T(8,128)S(1)}, f32[4,3,72,128]{3,2,1,0:T(8,128)S(1)}, u32[]{:S(2)}, u32[]{:S(2)}) %collective-permute-start.9) | collective-permute-done | bytes 442400 | tf_op jit(solution)/shard_map/c1_off/ppermute | solution.py:547
  112.2 3.7 %last1.1 = f32[8,4,64,128]{3,2,1,0:T(8,128)S(1)} custom-call(s32[1]{0:T(128)} %bitcast.parity_ref, f32[3,12,112,128]{3,2,1,0:T(8,128)S(1)} %get-tuple-element.29.coef_ref, f32[4,4,72,128]{3,2,1,0:T(8,128)S(1)} %get-tuple-element.40.own_in, f32[4,3,72,128]{3,2,1,0:T(8,128)S(1)} %collective-permute-done.8.on_in, ...), custom_call_target="tpu_custom_call" | custom-call | flops 5000000 | bytes 5000000 | tf_op jit(solution)/shard_map/last1/pallas_call | solution.py:550
  116.0 17.8 %all_to_all.11.back_ref = f32[4,2,4,64,128]{4,3,2,1,0:T(8,128)} all-to-all(f32[4,2,4,64,128]{4,3,2,1,0:T(8,128)S(1)} %bitcast.9), channel_id=1, replica_groups=mesh['tm'=4,'gx'=8] {'tm'}, dimensions={0} | all-to-all | bytes 2097152 | tf_op jit(solution)/shard_map/back/all_to_all | solution.py:663
  133.8 2.4 %finish.1 = f32[2,4,256,128]{3,2,1,0:T(8,128)} custom-call(f32[2]{0:T(128)} %weights_ref.3, f32[2,4,256,128]{3,2,1,0:T(8,128)} %state_ref.3, f32[4,2,4,64,128]{4,3,2,1,0:T(8,128)} %all_to_all.11.back_ref), custom_call_target="tpu_custom_call" | custom-call | tf_op jit(solution)/shard_map/finish/pallas_call | solution.py:670
  (19 shorter events, 0.7 us)
Async XLA Ops:
  2.3 49.8 %copy-start = (f32[8]{0:T(128)S(1)}, f32[8]{0:T(128)}, u32[]{:S(2)}) copy-start(f32[8]{0:T(128)} %shift_real_ref.1) | copy-start | bytes 100
  2.3 49.8 %copy-start.1 = (f32[8]{0:T(128)S(1)}, f32[8]{0:T(128)}, u32[]{:S(2)}) copy-start(f32[8]{0:T(128)} %shift_imag_ref.1) | copy-start | bytes 100
  26.0 26.1 %collective-permute-start = (f32[8,4,96,128]{3,2,1,0:T(8,128)S(1)}, f32[8,4,96,128]{3,2,1,0:T(8,128)}, u32[]{:S(2)}, u32[]{:S(2)}) collective-permute-start(f32[8,4,96,128]{3,2,1,0:T(8,128)S(1)} %bitcast.5), channel_id=1, source_target_pairs={{0,1},{1,0},{2,3},{3,2},{4,5},{5,4},{6,7},{7,6},{8,9},{9,8},{10,11... | collective-permute-start | bytes 4718600 | tf_op jit(solution)/shard_map/state_on/ppermute | solution.py:543
  26.0 33.1 %collective-permute-start.3 = (f32[8,4,96,128]{3,2,1,0:T(8,128)S(1)}, f32[8,4,96,128]{3,2,1,0:T(8,128)S(1)}, u32[]{:S(2)}, u32[]{:S(2)}) collective-permute-start(f32[8,4,96,128]{3,2,1,0:T(8,128)S(1)} %bitcast.6), channel_id=1, source_target_pairs={{1,2},{2,1},{3,4},{4,3},{5,6},{6,5},{9,10},{10,9},{11,12},{12,11},... | collective-permute-start | bytes 4718600 | tf_op jit(solution)/shard_map/state_off/ppermute | solution.py:547
  29.5 22.5 %collective-permute-start.2 = (f32[2,4,96,128]{3,2,1,0:T(8,128)S(1)}, f32[2,4,96,128]{3,2,1,0:T(8,128)}, u32[]{:S(2)}, u32[]{:S(2)}) collective-permute-start(f32[2,4,96,128]{3,2,1,0:T(8,128)S(1)} %fusion.1.fixed_own), channel_id=1, source_target_pairs={{1,2},{2,1},{3,4},{4,3},{5,6},{6,5},{9,10},{10,9},{11,12},{12,11},... | collective-permute-start | bytes 1179656 | tf_op jit(solution)/shard_map/fixed_off/ppermute | solution.py:547
  32.6 19.4 %collective-permute-start.1 = (f32[2,4,96,128]{3,2,1,0:T(8,128)S(1)}, f32[2,4,96,128]{3,2,1,0:T(8,128)}, u32[]{:S(2)}, u32[]{:S(2)}) collective-permute-start(f32[2,4,96,128]{3,2,1,0:T(8,128)S(1)} %fusion.1.fixed_own), channel_id=1, source_target_pairs={{0,1},{1,0},{2,3},{3,2},{4,5},{5,4},{6,7},{7,6},{8,9},{9,8},{10,11... | collective-permute-start | bytes 1179656 | tf_op jit(solution)/shard_map/fixed_on/ppermute | solution.py:543
  66.3 10.4 %collective-permute-start.10 = (f32[4,3,80,128]{3,2,1,0:T(8,128)S(1)}, f32[4,3,80,128]{3,2,1,0:T(8,128)S(1)}, u32[]{:S(2)}, u32[]{:S(2)}) collective-permute-start(f32[4,3,80,128]{3,2,1,0:T(8,128)S(1)} %get-tuple-element.45), channel_id=1, source_target_pairs={{0,1},{1,0},{2,3},{3,2},{4,5},{5,4},{6,7},{7,6},{8,9},{9,8},{10,11... | collective-permute-start | bytes 1474568 | tf_op jit(solution)/shard_map/a0_on/ppermute | solution.py:543
  66.9 10.1 %collective-permute-start.11 = (f32[4,3,80,128]{3,2,1,0:T(8,128)S(1)}, f32[4,3,80,128]{3,2,1,0:T(8,128)S(1)}, u32[]{:S(2)}, u32[]{:S(2)}) collective-permute-start(f32[4,3,80,128]{3,2,1,0:T(8,128)S(1)} %get-tuple-element.46), channel_id=1, source_target_pairs={{1,2},{2,1},{3,4},{4,3},{5,6},{6,5},{9,10},{10,9},{11,12},{12,11},... | collective-permute-start | bytes 1474568 | tf_op jit(solution)/shard_map/a0_off/ppermute | solution.py:547
  73.1 10.6 %collective-permute-start.4 = (f32[4,3,80,128]{3,2,1,0:T(8,128)S(1)}, f32[4,3,80,128]{3,2,1,0:T(8,128)S(1)}, u32[]{:S(2)}, u32[]{:S(2)}) collective-permute-start(f32[4,3,80,128]{3,2,1,0:T(8,128)S(1)} %get-tuple-element.35), channel_id=1, source_target_pairs={{0,1},{1,0},{2,3},{3,2},{4,5},{5,4},{6,7},{7,6},{8,9},{9,8},{10,11... | collective-permute-start | bytes 1474568 | tf_op jit(solution)/shard_map/a1_on/ppermute | solution.py:543
  74.3 10.1 %collective-permute-start.5 = (f32[4,3,80,128]{3,2,1,0:T(8,128)S(1)}, f32[4,3,80,128]{3,2,1,0:T(8,128)S(1)}, u32[]{:S(2)}, u32[]{:S(2)}) collective-permute-start(f32[4,3,80,128]{3,2,1,0:T(8,128)S(1)} %get-tuple-element.36), channel_id=1, source_target_pairs={{1,2},{2,1},{3,4},{4,3},{5,6},{6,5},{9,10},{10,9},{11,12},{12,11},... | collective-permute-start | bytes 1474568 | tf_op jit(solution)/shard_map/a1_off/ppermute | solution.py:547
  80.8 10.4 %collective-permute-start.12 = (f32[4,3,80,128]{3,2,1,0:T(8,128)S(1)}, f32[4,3,80,128]{3,2,1,0:T(8,128)S(1)}, u32[]{:S(2)}, u32[]{:S(2)}) collective-permute-start(f32[4,3,80,128]{3,2,1,0:T(8,128)S(1)} %get-tuple-element.48), channel_id=1, source_target_pairs={{0,1},{1,0},{2,3},{3,2},{4,5},{5,4},{6,7},{7,6},{8,9},{9,8},{10,11... | collective-permute-start | bytes 1474568 | tf_op jit(solution)/shard_map/b0_on/ppermute | solution.py:543
  80.9 10.2 %collective-permute-start.13 = (f32[4,3,80,128]{3,2,1,0:T(8,128)S(1)}, f32[4,3,80,128]{3,2,1,0:T(8,128)S(1)}, u32[]{:S(2)}, u32[]{:S(2)}) collective-permute-start(f32[4,3,80,128]{3,2,1,0:T(8,128)S(1)} %get-tuple-element.49), channel_id=1, source_target_pairs={{1,2},{2,1},{3,4},{4,3},{5,6},{6,5},{9,10},{10,9},{11,12},{12,11},... | collective-permute-start | bytes 1474568 | tf_op jit(solution)/shard_map/b0_off/ppermute | solution.py:547
  88.1 10.0 %collective-permute-start.6 = (f32[4,3,80,128]{3,2,1,0:T(8,128)S(1)}, f32[4,3,80,128]{3,2,1,0:T(8,128)S(1)}, u32[]{:S(2)}, u32[]{:S(2)}) collective-permute-start(f32[4,3,80,128]{3,2,1,0:T(8,128)S(1)} %get-tuple-element.38), channel_id=1, source_target_pairs={{0,1},{1,0},{2,3},{3,2},{4,5},{5,4},{6,7},{7,6},{8,9},{9,8},{10,11... | collective-permute-start | bytes 1474568 | tf_op jit(solution)/shard_map/b1_on/ppermute | solution.py:543
  88.3 10.1 %collective-permute-start.7 = (f32[4,3,80,128]{3,2,1,0:T(8,128)S(1)}, f32[4,3,80,128]{3,2,1,0:T(8,128)S(1)}, u32[]{:S(2)}, u32[]{:S(2)}) collective-permute-start(f32[4,3,80,128]{3,2,1,0:T(8,128)S(1)} %get-tuple-element.39), channel_id=1, source_target_pairs={{1,2},{2,1},{3,4},{4,3},{5,6},{6,5},{9,10},{10,9},{11,12},{12,11},... | collective-permute-start | bytes 1474568 | tf_op jit(solution)/shard_map/b1_off/ppermute | solution.py:547
  94.9 10.3 %collective-permute-start.14 = (f32[4,3,72,128]{3,2,1,0:T(8,128)S(1)}, f32[4,3,72,128]{3,2,1,0:T(8,128)S(1)}, u32[]{:S(2)}, u32[]{:S(2)}) collective-permute-start(f32[4,3,72,128]{3,2,1,0:T(8,128)S(1)} %get-tuple-element.51), channel_id=1, source_target_pairs={{0,1},{1,0},{2,3},{3,2},{4,5},{5,4},{6,7},{7,6},{8,9},{9,8},{10,11... | collective-permute-start | bytes 1327112 | tf_op jit(solution)/shard_map/c0_on/ppermute | solution.py:543
  95.3 9.9 %collective-permute-start.15 = (f32[4,3,72,128]{3,2,1,0:T(8,128)S(1)}, f32[4,3,72,128]{3,2,1,0:T(8,128)S(1)}, u32[]{:S(2)}, u32[]{:S(2)}) collective-permute-start(f32[4,3,72,128]{3,2,1,0:T(8,128)S(1)} %get-tuple-element.52), channel_id=1, source_target_pairs={{1,2},{2,1},{3,4},{4,3},{5,6},{6,5},{9,10},{10,9},{11,12},{12,11},... | collective-permute-start | bytes 1327112 | tf_op jit(solution)/shard_map/c0_off/ppermute | solution.py:547
  102.2 6.8 %collective-permute-start.8 = (f32[4,3,72,128]{3,2,1,0:T(8,128)S(1)}, f32[4,3,72,128]{3,2,1,0:T(8,128)S(1)}, u32[]{:S(2)}, u32[]{:S(2)}) collective-permute-start(f32[4,3,72,128]{3,2,1,0:T(8,128)S(1)} %get-tuple-element.41), channel_id=1, source_target_pairs={{0,1},{1,0},{2,3},{3,2},{4,5},{5,4},{6,7},{7,6},{8,9},{9,8},{10,11... | collective-permute-start | bytes 1327112 | tf_op jit(solution)/shard_map/c1_on/ppermute | solution.py:543
  102.6 9.6 %collective-permute-start.9 = (f32[4,3,72,128]{3,2,1,0:T(8,128)S(1)}, f32[4,3,72,128]{3,2,1,0:T(8,128)S(1)}, u32[]{:S(2)}, u32[]{:S(2)}) collective-permute-start(f32[4,3,72,128]{3,2,1,0:T(8,128)S(1)} %get-tuple-element.42), channel_id=1, source_target_pairs={{1,2},{2,1},{3,4},{4,3},{5,6},{6,5},{9,10},{10,9},{11,12},{12,11},... | collective-permute-start | bytes 1327112 | tf_op jit(solution)/shard_map/c1_off/ppermute | solution.py:547

commit v3 on v2

--- a/solution.py
+++ b/solution.py
@@ -9,8 +9,8 @@
 from jax.experimental.pallas import tpu as pltpu
 from jax.sharding import PartitionSpec as P
 
+
 SWEEPS = 12
-DEPTH = 3
 YHALO = 16
 PAD = 8
 GROUPS = 2
@@ -125,9 +125,8 @@
 
 
 def sweeps_on(buffers, coef_ref, w0_ref, inv_ref, pair, done, block, rows):
-    own = DEPTH + 1
-    for step in range(DEPTH):
-        reach = DEPTH - 1 - step
+    for step in range(block):
+        reach = block - 1 - step
         sweep(
             buffers[step % 2],
             buffers[(step + 1) % 2],
@@ -136,36 +135,20 @@
             inv_ref,
             pair,
             omegas()[done + step],
-            (own - reach, block + 2 * reach),
+            (block - reach, block + 2 * reach),
             chunks_of(rows, SWEEPS - 1 - done - step),
         )
-    return buffers[DEPTH % 2]
-
-
-def send_out(result, pair, parity, own_ref, on_ref, off_ref, block, own_window, window):
-    own = DEPTH + 1
-    first_on = own + jnp.where(parity == 0, block - DEPTH, 0)
-    first_off = own + jnp.where(parity == 0, 0, block - DEPTH)
-    own_at = pl.ds(PAD + own_window[0], own_window[1])
+    return buffers[block % 2]
+
+
+def load_in(buffer_a, pair, parity, own_ref, on_ref, off_ref, window):
+    block = own_ref.shape[1]
     at = pl.ds(PAD + window[0], window[1])
-    for which in range(2):
-        for plane in range(DEPTH):
-            off_ref[2 * pair + which, plane] = result[which, first_off + plane, at, :]
-            on_ref[2 * pair + which, plane] = result[which, first_on + plane, at, :]
-        for plane in range(block):
-            own_ref[2 * pair + which, plane] = result[which, own + plane, own_at, :]
-
-
-def load_in(buffer_a, pair, parity, own_ref, on_ref, off_ref, block, own_window, window):
-    own = DEPTH + 1
-    own_at = pl.ds(PAD + own_window[0], own_window[1])
-    at = pl.ds(PAD + window[0], window[1])
-    first_on = jnp.where(parity == 0, own + block, 1)
-    first_off = jnp.where(parity == 0, 1, own + block)
+    first_on = jnp.where(parity == 0, 2 * block, 0)
+    first_off = jnp.where(parity == 0, 0, 2 * block)
     for which in range(2):
         for plane in range(block):
-            buffer_a[which, own + plane, own_at, :] = own_ref[2 * pair + which, plane]
-        for plane in range(DEPTH):
+            buffer_a[which, block + plane, at, :] = own_ref[2 * pair + which, plane]
             buffer_a[which, first_on + plane, at, :] = on_ref[2 * pair + which, plane]
             buffer_a[which, first_off + plane, at, :] = off_ref[2 * pair + which, plane]
 
@@ -217,7 +200,7 @@
             out_ref[0, plane, at, :] = state_ref[0, plane, at, :] + back_ref[piece, 0, plane] * scale
 
 
-def residual_starts(wide, base, planes, state_own, field_of, coef_ref, diag_ref, inv_ref, w0_refs):
+def residual_starts(wide, base, planes, state_own, field_of, coef_ref, diag_ref, inv_ref, w0_ref, w0_base):
     total = wide.shape[0]
     rows = diag_ref.shape[1]
     half = total // 2
@@ -246,16 +229,23 @@
                 cross = inv_ref[3 * pair + 2, plane - 1, at, :]
                 w_a = inv_a * spec_a - cross * spec_b
                 w_b = inv_b * spec_b + cross * spec_a
-                put(w0_refs, 2 * pair, plane - 1, at, w_a)
-                put(w0_refs, 2 * pair + 1, plane - 1, at, w_b)
+                w0_ref[2 * pair, plane - w0_base, at, :] = w_a
+                w0_ref[2 * pair + 1, plane - w0_base, at, :] = w_b
         return 0
 
     lax.fori_loop(0, count, one, 0)
 
 
-def put(refs, lead, plane, at, value):
-    per = refs[0].shape[0]
-    refs[lead // per][lead % per, plane, at, :] = value
+def edges_kernel(parity_ref, state_ref, on_ref, off_ref):
+    block = state_ref.shape[1]
+    near_on = jnp.where(parity_ref[0] == 0, block - 1, 0)
+
+    def one(lead, _):
+        on_ref[lead, 0] = state_ref[lead, near_on]
+        off_ref[lead, 0] = state_ref[lead, block - 1 - near_on]
+        return 0
+
+    lax.fori_loop(0, state_ref.shape[0], one, 0)
 
 
 def early_kernel(
@@ -276,22 +266,22 @@
 ):
     total, block, rows, lanes = state_own.shape
     half = total // 2
-    own = DEPTH + 1
-    planes = block + 2 * own
+    planes = 3 * block
     parity = parity_ref[0]
-    first_on = jnp.where(parity == 0, own + block, 0)
-    first_off = jnp.where(parity == 0, 0, own + block)
-    base = jnp.where(parity == 0, own, 0)
+    first_on = jnp.where(parity == 0, 2 * block, 0)
+    first_off = jnp.where(parity == 0, 0, 2 * block)
+    base = jnp.where(parity == 0, block, block - 1)
     clear_edges((fixed, coef_ref), rows, 0)
     clear_edges((wide,), rows, 0)
     body = pl.ds(PAD, rows)
+    for lead in range(total):
+        wide[lead, jnp.where(parity == 0, block, 0), body, :] = state_on[lead, 0]
 
     def place(plane, _):
         for lead in range(total):
-            wide[lead, own - base + plane, body, :] = state_own[lead, plane]
-            wide[lead, first_on - base + plane, body, :] = state_on[lead, plane]
+            wide[lead, block - base + plane, body, :] = state_own[lead, plane]
         for lead in range(2):
-            fixed[lead, own + plane, body, :] = fixed_own[lead, plane]
+            fixed[lead, block + plane, body, :] = fixed_own[lead, plane]
             fixed[lead, first_on + plane, body, :] = fixed_on[lead, plane]
             fixed[lead, first_off + plane, body, :] = fixed_off[lead, plane]
         return 0
@@ -346,152 +336,101 @@
     def field_of(plane, row):
         return fixed[0, plane, pl.ds(row, 8), :]
 
-    count = block + own - 2
-    first = jnp.where(parity == 0, planes - 1 - count, 1)
+    first = jnp.where(parity == 0, block + 1, block)
     residual_starts(
-        wide, base, (first, count), state_own, field_of, coef_ref, diag_ref, inv_ref, (w0_ref,)
+        wide, base, (first, block - 1), state_own, field_of, coef_ref, diag_ref, inv_ref, w0_ref, block
     )
 
 
 def late_kernel(
-    parity_ref,
-    state_own,
-    state_off,
-    fixed_own,
-    fixed_off,
-    coef_ref,
-    diag_ref,
-    inv_ref,
-    w0_in,
-    *rest,
+    window, parity_ref, state_own, state_off, fixed_own, coef_ref, diag_ref, inv_ref, w0_in, *rest
 ):
-    w0_refs, wide, field = rest[:-2], rest[-2], rest[-1]
-    total, block, rows, lanes = state_own.shape
-    own = DEPTH + 1
-    planes = block + 2 * own
+    w0_refs, wide, outer = rest[:-2], rest[-2], rest[-1]
+    total, block, rows, _ = state_own.shape
     parity = parity_ref[0]
-    base = jnp.where(parity == 0, 0, planes - own - 2)
-    first_off = jnp.where(parity == 0, 0, 2)
-    first_own = jnp.where(parity == 0, own, 0)
+    base = jnp.where(parity == 0, block - 1, 2 * block - 2)
+    at_off = jnp.where(parity == 0, 0, 2)
+    at_own = jnp.where(parity == 0, 1, 0)
     from_own = jnp.where(parity == 0, 0, block - 2)
     clear_edges((wide,), rows, 0)
     body = pl.ds(PAD, rows)
-
-    def place_off(plane, _):
-        for lead in range(total):
-            wide[lead, first_off + plane, body, :] = state_off[lead, plane]
-        field[first_off + plane, body, :] = fixed_off[0, plane]
-        return 0
-
-    def place_own(plane, _):
-        for lead in range(total):
-            wide[lead, first_own + plane, body, :] = state_own[lead, from_own + plane]
-        field[first_own + plane, body, :] = fixed_own[0, from_own + plane]
-        return 0
-
-    lax.fori_loop(0, block, place_off, 0)
-    lax.fori_loop(0, 2, place_own, 0)
-    count = block + own - 2
-    first = jnp.where(parity == 0, planes - 1 - count, 1)
-
-    def copy(turn, _):
-        for lead in range(total):
-            put(w0_refs, lead, first - 1 + turn, slice(None), w0_in[lead, first - 1 + turn])
-        return 0
-
-    lax.fori_loop(0, count, copy, 0)
+    for lead in range(total):
+        wide[lead, at_off, body, :] = state_off[lead, 0]
+        wide[lead, at_own, body, :] = state_own[lead, from_own]
+        wide[lead, at_own + 1, body, :] = state_own[lead, from_own + 1]
 
     def field_of(plane, row):
-        return field[plane - base, pl.ds(row, 8), :]
+        return fixed_own[0, plane - block, pl.ds(row - PAD, 8), :]
 
     residual_starts(
-        wide, base, (base + 1, own), state_own, field_of, coef_ref, diag_ref, inv_ref, w0_refs
+        wide,
+        base,
+        (base + 1, 1),
+        state_own,
+        field_of,
+        coef_ref,
+        diag_ref,
+        inv_ref,
+        outer,
+        base + 1,
     )
-
-
-def first_kernel(
-    low_pair,
-    own_window,
-    window,
-    parity_ref,
-    coef_ref,
-    w0_ref,
-    inv_ref,
-    own_ref,
-    on_ref,
-    off_ref,
-    buffer_a,
-    buffer_b,
+    inner = jnp.where(parity == 0, 1, 0)
+    outermost = jnp.where(parity == 0, 0, block - 1)
+    per = w0_refs[0].shape[0]
+    at = pl.ds(*window)
+    for group in range(len(w0_refs)):
+        for lead in range(per):
+            source = group * per + lead
+            for plane in range(block - 1):
+                w0_refs[group][lead, inner + plane] = w0_in[source, inner + plane, at, :]
+            w0_refs[group][lead, outermost] = outer[source, 0, at, :]
+
+
+def phase_kernel(
+    low_pair, done, window, next_window, parity_ref, coef_ref, inv_ref, own_in, on_in, off_in, *rest
 ):
+    buffer_a, buffer_b = rest[-2:]
+    if done == 0:
+        w0_ref, out_ref = rest[:2]
+    else:
+        w0_ref, out_ref = rest[0], rest[1]
     parity = parity_ref[0]
-    block = own_ref.shape[1]
-    rows = w0_ref.shape[2]
-    clear_edges((buffer_a, buffer_b), rows, 0)
-    group_inv = inv_ref.at[pl.ds(3 * low_pair, 3 * (w0_ref.shape[0] // 2))]
+    pairs, block, rows = w0_ref.shape[0] // 2, own_in.shape[1], w0_ref.shape[2]
+    clear_edges((buffer_a, buffer_b), rows, window[0])
+    group_inv = inv_ref.at[pl.ds(3 * low_pair, 3 * pairs)]
 
     def one(pair, _):
-        def copy(plane, _):
-            for which in range(2):
-                buffer_a[which, plane + 1, pl.ds(PAD, rows), :] = w0_ref[2 * pair + which, plane]
-            return 0
-
-        lax.fori_loop(0, w0_ref.shape[1], copy, 0)
-        result = sweeps_on((buffer_a, buffer_b), coef_ref, w0_ref, group_inv, pair, 0, block, rows)
-        send_out(result, pair, parity, own_ref, on_ref, off_ref, block, own_window, window)
-        return 0
-
-    lax.fori_loop(0, w0_ref.shape[0] // 2, one, 0)
-
-
-def middle_kernel(
-    low_pair,
-    done,
-    windows,
-    next_windows,
-    parity_ref,
-    coef_ref,
-    own_in,
-    on_in,
-    off_in,
-    w0_ref,
-    inv_ref,
-    own_ref,
-    on_ref,
-    off_ref,
-    buffer_a,
-    buffer_b,
-):
-    parity = parity_ref[0]
-    block = own_in.shape[1]
-    rows = w0_ref.shape[2]
-    clear_edges((buffer_a, buffer_b), rows, 16)
-    group_inv = inv_ref.at[pl.ds(3 * low_pair, 3 * (w0_ref.shape[0] // 2))]
-
-    def one(pair, _):
-        load_in(buffer_a, pair, parity, own_in, on_in, off_in, block, *windows)
+        load_in(buffer_a, pair, parity, own_in, on_in, off_in, window)
+        if done == 0:
+
+            def keep(plane, _):
+                for which in range(2):
+                    w0_ref[2 * pair + which, plane] = buffer_a[which, plane + 1, pl.ds(PAD, rows), :]
+                return 0
+
+            lax.fori_loop(0, w0_ref.shape[1], keep, 0)
         result = sweeps_on((buffer_a, buffer_b), coef_ref, w0_ref, group_inv, pair, done, block, rows)
-        send_out(result, pair, parity, own_ref, on_ref, off_ref, block, *next_windows)
-        return 0
-
-    lax.fori_loop(0, w0_ref.shape[0] // 2, one, 0)
-
-
-def last_kernel(low_pair, done, windows, parity_ref, coef_ref, own_in, on_in, off_in, w0_ref, inv_ref, *rest):
+        at = pl.ds(PAD + next_window[0], next_window[1])
+        for which in range(2):
+            for plane in range(block):
+                out_ref[2 * pair + which, plane] = result[which, block + plane, at, :]
+        return 0
+
+    lax.fori_loop(0, pairs, one, 0)
+
+
+def last_kernel(low_pair, done, window, parity_ref, coef_ref, inv_ref, own_in, on_in, off_in, w0_ref, *rest):
     out_ref, buffer_a, buffer_b = rest[-3:]
     parity = parity_ref[0]
-    block = own_in.shape[1]
-    rows = w0_ref.shape[2]
+    pairs, block, rows = w0_ref.shape[0] // 2, own_in.shape[1], w0_ref.shape[2]
     total, chunk_rows = out_ref.shape[0], out_ref.shape[2]
-    pairs = w0_ref.shape[0] // 2
-    own = DEPTH + 1
-    clear_edges((buffer_a, buffer_b), rows, 16)
+    clear_edges((buffer_a, buffer_b), rows, window[0])
     group_inv = inv_ref.at[pl.ds(3 * low_pair, 3 * pairs)]
     table = mode_terms(total).T / total
     table[:, 2:] *= 2.0
-    half = total // 2
     for pair in range(pairs):
         mode = low_pair + pair
-        load_in(buffer_a, pair, parity, own_in, on_in, off_in, block, *windows)
+        load_in(buffer_a, pair, parity, own_in, on_in, off_in, window)
         result = sweeps_on((buffer_a, buffer_b), coef_ref, w0_ref, group_inv, pair, done, block, rows)
         before = None
         if pair > 0:
@@ -503,8 +442,8 @@
             for chunk in range(chunk_rows // 8):
                 at = pl.ds(8 * chunk, 8)
                 row = pl.ds(PAD + YHALO + 8 * chunk, 8)
-                w_a = result[0, own + plane, row, :]
-                w_b = result[1, own + plane, row, :]
+                w_a = result[0, block + plane, row, :]
+                w_b = result[1, block + plane, row, :]
                 for lead in range(total):
                     value = weighted((w_a, w_b), table[lead, 2 * mode : 2 * mode + 2])
                     if before is not None:
@@ -524,8 +463,7 @@
     per = pairs // GROUPS
     chunk = length // pieces
     rows = chunk + 2 * YHALO
-    own = DEPTH + 1
-    planes = block + 2 * own
+    planes = 3 * block
     padded = rows + 2 * PAD
     f32 = jnp.float32
     device = lax.axis_index("tm")
@@ -538,15 +476,13 @@
     def shape(*dims):
         return jax.ShapeDtypeStruct(dims, f32)
 
-    def swap_on(value, name):
-        with jax.named_scope(f"{name}_on"):
-            return lax.ppermute(value, "gx", on_pairs)
-
-    def swap_off(value, name):
-        with jax.named_scope(f"{name}_off"):
-            return lax.ppermute(value, "gx", off_pairs)
-
-    def call(kernel, name, inputs, scalars, outs, scratch, flops):
+    def swap_on(value):
+        return lax.ppermute(value, "gx", on_pairs)
+
+    def swap_off(value):
+        return lax.ppermute(value, "gx", off_pairs)
+
+    def call(kernel, inputs, scalars, outs, scratch, flops):
         return pl.pallas_call(
             kernel,
             in_specs=[SMEM] * scalars + [VMEM] * (len(inputs) - scalars),
@@ -555,13 +491,12 @@
             scratch_shapes=[pltpu.VMEM(dims, f32) for dims in scratch],
             compiler_params=pltpu.CompilerParams(vmem_limit_bytes=LIMIT),
             cost_estimate=pl.CostEstimate(flops=flops, bytes_accessed=flops, transcendentals=0),
-            name=name,
         )(*inputs)
 
     fixed = jnp.pad(jnp.stack([start_field, diffusivity]), ((0, 0), (0, 0), (YHALO, YHALO), (0, 0)))
     fixed = lax.dynamic_slice_in_dim(fixed, device * chunk, rows, axis=2)
-    fixed_off = swap_off(fixed, "fixed")
-    fixed_on = swap_on(fixed, "fixed")
+    fixed_off = swap_off(fixed)
+    fixed_on = swap_on(fixed)
 
     step_spec = pl.BlockSpec((1, block, length, lanes), lambda i: (i, 0, 0, 0))
     packed = pl.pallas_call(
@@ -572,101 +507,85 @@
         out_shape=shape(pieces, steps, block, rows, lanes),
         name="pack",
     )(time_weights, state)
-    with jax.named_scope("mix"):
-        mixed = lax.all_to_all(packed, "tm", split_axis=0, concat_axis=0, tiled=True)
+    mixed = lax.all_to_all(packed, "tm", split_axis=0, concat_axis=0, tiled=True)
     mixed = mixed.reshape((total, block, rows, lanes))
-    mixed_off = swap_off(mixed, "state")
-    mixed_on = swap_on(mixed, "state")
-
-    def window_of(halo):
-        low = (YHALO - halo) // 4 * 4
-        return low, rows - 2 * low
+    edge = shape(total, 1, rows, lanes)
+    edge_on, edge_off = call(edges_kernel, (parity, mixed), 1, [edge] * 2, [], COST // 10)
+    mixed_off = swap_off(edge_off)
+    mixed_on = swap_on(edge_on)
 
     windows = []
-    for phase in range(1, SWEEPS // DEPTH):
-        left = SWEEPS - DEPTH * phase
-        windows.append((window_of(left), window_of(left - 1)))
+    for left in range(SWEEPS, 0, -block):
+        low = (YHALO - left) // 4 * 4
+        windows.append((low, rows - 2 * low))
 
     coefs, diag, inverse, w0 = call(
         early_kernel,
-        "early",
         (parity, shift_real, shift_imag, mixed, mixed_on, fixed, fixed_on, fixed_off),
         3,
         [
             shape(3, planes, padded, lanes),
             shape(planes - 2, rows, lanes),
             shape(3 * pairs, planes - 2, rows, lanes),
-            shape(total, planes - 2, rows, lanes),
+            shape(total, block, rows, lanes),
         ],
-        [(total, planes - own, padded, lanes), (2, planes, padded, lanes)],
+        [(total, block + 1, padded, lanes), (2, planes, padded, lanes)],
         COST,
     )
-    starts = call(
-        late_kernel,
-        "late",
-        (parity, mixed, mixed_off, fixed, fixed_off, coefs, diag, inverse, w0),
+    values = call(
+        functools.partial(late_kernel, windows[0]),
+        (parity, mixed, mixed_off, fixed, coefs, diag, inverse, w0),
         1,
-        [shape(2 * per, planes - 2, rows, lanes)] * GROUPS,
-        [(total, own + 2, padded, lanes), (own + 2, padded, lanes)],
-        COST,
+        [shape(2 * per, block, windows[0][1], lanes)] * GROUPS,
+        [(total, 3, padded, lanes), (total, 1, rows, lanes)],
+        COST // 4,
     )
     buffers = [(2, planes, padded, lanes)] * 2
 
-    def sent(pair_windows):
-        own_window, window = pair_windows
-        return [
-            shape(2 * per, block, own_window[1], lanes),
-            shape(2 * per, DEPTH, window[1], lanes),
-            shape(2 * per, DEPTH, window[1], lanes),
-        ]
-
-    moving = []
-    for group in range(GROUPS):
-        own_w, on_w, off_w = call(
-            functools.partial(first_kernel, per * group, *windows[0]),
-            f"first{group}",
-            (parity, coefs, starts[group], inverse),
-            1,
-            sent(windows[0]),
-            buffers,
-            COST,
-        )
-        moving.append((own_w, swap_on(on_w, f"a{group}"), swap_off(off_w, f"a{group}")))
-    last = SWEEPS // DEPTH - 1
-    for phase in range(1, last):
+    def exchange(value):
+        return value, swap_on(value), swap_off(value)
+
+    moving = [exchange(values[group]) for group in range(GROUPS)]
+    starts = [None] * GROUPS
+    last = len(windows) - 1
+    for phase in range(last):
         for group in range(GROUPS):
-            own_w, on_w, off_w = call(
+            outs = [shape(2 * per, block, windows[phase + 1][1], lanes)]
+            extra = ()
+            if phase == 0:
+                outs = [shape(2 * per, planes - 2, rows, lanes)] + outs
+            else:
+                extra = (starts[group],)
+            results = call(
                 functools.partial(
-                    middle_kernel, per * group, DEPTH * phase, windows[phase - 1], windows[phase]
+                    phase_kernel, per * group, block * phase, windows[phase], windows[phase + 1]
                 ),
-                f"middle{phase}{group}",
-                (parity, coefs, *moving[group], starts[group], inverse),
+                (parity, coefs, inverse, *moving[group], *extra),
                 1,
-                sent(windows[phase]),
+                outs,
                 buffers,
                 COST,
             )
-            name = "abcdefgh"[phase] + str(group)
-            moving[group] = (own_w, swap_on(on_w, name), swap_off(off_w, name))
+            if phase == 0:
+                starts[group] = results[0]
+            moving[group] = exchange(results[-1])
     delta = ()
     for group in range(GROUPS):
         delta = call(
-            functools.partial(last_kernel, per * group, DEPTH * last, windows[last - 1]),
-            f"last{group}",
-            (parity, coefs, *moving[group], starts[group], inverse, *delta),
+            functools.partial(last_kernel, per * group, block * last, windows[last]),
+            (parity, coefs, inverse, *moving[group], starts[group], *delta),
             1,
             [shape(total, block, chunk, lanes)],
             buffers,
             COST,
         )
-    with jax.named_scope("back"):
-        back = lax.all_to_all(
-            delta[0].reshape((pieces, steps, block, chunk, lanes)),
-            "tm",
-            split_axis=0,
-            concat_axis=0,
-            tiled=True,
-        )
+    back = lax.all_to_all(
+        delta[0].reshape((pieces, steps, block, chunk, lanes)),
+        "tm",
+        split_axis=0,
+        concat_axis=0,
+        tiled=True,
+    )
     return pl.pallas_call(
         finish_kernel,
         grid=(steps,),

time: 137 us -> 118 us (0.86)
  blocking collectives: 41.5 us -> 18.1 us
  waiting for transfers between devices: 23.5 us -> 30.7 us
  Pallas kernels: 45.4 us -> 40.2 us
  starting transfers between devices: 24.4 us -> 26.9 us
    all_to_all x1 -> x0, blocking collectives: 23.7 us -> none  [shards(): lax.all_to_all(packed, 'tm', split_axis=0, concat_axis=0, tiled=True)]
    all_to_all x0 -> x1, waiting for transfers between devices: none -> 16.7 us  [shards(): lax.all_to_all(packed, 'tm', split_axis=0, concat_axis=0, tiled=True)]
    ppermute x8, waiting for transfers between devices: 23.5 us -> 14 us  [swap_off(): return lax.ppermute(value, 'gx', off_pairs)]
    pallas_call x10 -> x9, Pallas kernels: 40.8 us -> 35.6 us  [call(): pl.pallas_call(kernel, in_specs=[SMEM] * scalars + [VMEM] * (len(inputs)...]
    all_to_all x0 -> x1, starting transfers between devices: none -> 3.85 us  [shards(): lax.all_to_all(packed, 'tm', split_axis=0, concat_axis=0, tiled=True)]
  transfers between devices with their start and end apart: 16 -> 17, of which waited for: 5 -> 6; matrix products, arithmetic and copies ran while one was open for 1% -> 0% of each run, Pallas kernels for 22% -> 26%
where the time goes in v3:
time: 118 us; the launch traced here: 116 us
  Pallas kernels  40.2 us (34%)
  waiting for transfers between devices  30.7 us (26%)
  starting transfers between devices  26.9 us (23%)
  blocking collectives  18.1 us (15%)
    pallas_call x9, Pallas kernels, call(): pl.pallas_call(kernel, in_specs=[SMEM] * scalars + [VMEM] * (len(inputs)...  35.6 us
    ppermute x8, starting transfers between devices, swap_off(): return lax.ppermute(value, 'gx', off_pairs)  19.5 us
    all_to_all x1, blocking collectives, shards(): lax.all_to_all(delta[0].reshape((pieces, steps, block, chunk, lanes)), 't...  18.1 us
    all_to_all x1, waiting for transfers between devices, shards(): lax.all_to_all(packed, 'tm', split_axis=0, concat_axis=0, tiled=True)  16.7 us
    ppermute x8, waiting for transfers between devices, swap_off(): return lax.ppermute(value, 'gx', off_pairs)  14 us
    all_to_all x1, starting transfers between devices, shards(): lax.all_to_all(packed, 'tm', split_axis=0, concat_axis=0, tiled=True)  3.85 us
    ppermute x8, starting transfers between devices, swap_on(): return lax.ppermute(value, 'gx', on_pairs)  3.49 us
    pallas_call x1, Pallas kernels, shards(): pl.pallas_call(finish_kernel, grid=(steps,), in_specs=[SMEM, step_spec, p...  2.38 us
  transfers between devices with their start and end apart: 17, of which 6 were waited for; matrix products, arithmetic and copies ran while one was open for 0% of the time, Pallas kernels for 26%

profile of v3, /device:TPU:16, one launch (start us, length us, event | category | flops | bytes accessed | tf_op | source)
XLA Modules:
  0.0 116.3 jit_solution(15171017177040648999)
XLA Ops:
  0.0 2.3 %pack.1 = f32[4,2,4,96,128]{4,3,2,1,0:T(8,128)} custom-call(f32[2]{0:T(128)} %weights_ref.3, f32[2,4,256,128]{3,2,1,0:T(8,128)} %state_ref.3), custom_call_target="tpu_custom_call" | custom-call | tf_op jit(solution)/shard_map/pack/pallas_call | solution.py:502
  2.3 3.8 %all-to-all-start = ((f32[4,2,4,96,128]{4,3,2,1,0:T(8,128)}), f32[4,2,4,96,128]{4,3,2,1,0:T(8,128)S(1)}, u32[]{:S(2)}, u32[]{:S(2)}) async-start(f32[4,2,4,96,128]{4,3,2,1,0:T(8,128)} %pack.1), calls=%async_computation | async-start | bytes 3145728 | tf_op jit(solution)/shard_map/all_to_all | solution.py:510
  6.3 2.4 %collective-permute-start.2 = (f32[2,4,96,128]{3,2,1,0:T(8,128)S(1)}, f32[2,4,96,128]{3,2,1,0:T(8,128)S(1)}, u32[]{:S(2)}, u32[]{:S(2)}) collective-permute-start(f32[2,4,96,128]{3,2,1,0:T(8,128)S(1)} %fusion.1.fixed_own), channel_id=1, source_target_pairs={{1,2},{2,1},{3,4},{4,3},{5,6},{6,5},{9,10},{10,9},{11,12},{12,11},... | collective-permute-start | bytes 1179656 | tf_op jit(solution)/shard_map/ppermute | solution.py:483
  8.7 16.7 %all-to-all-done = f32[4,2,4,96,128]{4,3,2,1,0:T(8,128)S(1)} async-done(((f32[4,2,4,96,128]{4,3,2,1,0:T(8,128)}), f32[4,2,4,96,128]{4,3,2,1,0:T(8,128)S(1)}, u32[]{:S(2)}, u32[]{:S(2)}) %all-to-all-start) | async-done | bytes 1572896 | tf_op jit(solution)/shard_map/all_to_all | solution.py:510
  25.6 2.4 %collective-permute-start.3 = (f32[8,1,96,128]{3,2,1,0:T(8,128)S(1)}, f32[8,1,96,128]{3,2,1,0:T(8,128)S(1)}, u32[]{:S(2)}, u32[]{:S(2)}) collective-permute-start(f32[8,1,96,128]{3,2,1,0:T(8,128)S(1)} %get-tuple-element.20), channel_id=1, source_target_pairs={{1,2},{2,1},{3,4},{4,3},{5,6},{6,5},{9,10},{10,9},{11,12},{12,11},... | collective-permute-start | bytes 1179656 | tf_op jit(solution)/shard_map/ppermute | solution.py:483
  28.1 4.5 %shard_map.65 = (f32[3,12,112,128]{3,2,1,0:T(8,128)S(1)}, f32[10,96,128]{2,1,0:T(8,128)S(1)}, f32[12,10,96,128]{3,2,1,0:T(8,128)S(1)}, f32[8,4,96,128]{3,2,1,0:T(8,128)S(1)}) custom-call(s32[1]{0:T(128)} %bitcast.parity_ref, f32[8]{0:T(128)S(1)} %copy-done, f32[8]{0:T(128)S(1)} %copy-done.1, f32[8,4,96,128]{3,2,1,0:T(8,128)S(1)} %bitcast.6, ...), custom_call_target="tpu_custom_call" | custom-call | flops 5000000 | bytes 5000000 | tf_op jit(solution)/shard_map/pallas_call | solution.py:486
  32.7 2.0 %collective-permute-done.3.state_off = f32[8,1,96,128]{3,2,1,0:T(8,128)S(1)} collective-permute-done((f32[8,1,96,128]{3,2,1,0:T(8,128)S(1)}, f32[8,1,96,128]{3,2,1,0:T(8,128)S(1)}, u32[]{:S(2)}, u32[]{:S(2)}) %collective-permute-start.3) | collective-permute-done | bytes 393248 | tf_op jit(solution)/shard_map/ppermute | solution.py:483
  34.7 0.8 shard_map.66
  35.5 0.5 collective-permute-start.10
  36.0 2.0 %collective-permute-start.11 = (f32[4,4,88,128]{3,2,1,0:T(8,128)S(1)}, f32[4,4,88,128]{3,2,1,0:T(8,128)S(1)}, u32[]{:S(2)}, u32[]{:S(2)}) collective-permute-start(f32[4,4,88,128]{3,2,1,0:T(8,128)S(1)} %get-tuple-element.26.own_in), channel_id=1, source_target_pairs={{1,2},{2,1},{3,4},{4,3},{5,6},{6,5},{9,10},{10,9},{11,12},{12,11},... | collective-permute-start | bytes 2162696 | tf_op jit(solution)/shard_map/ppermute | solution.py:483
  38.0 1.2 %collective-permute-start.4 = (f32[4,4,88,128]{3,2,1,0:T(8,128)S(1)}, f32[4,4,88,128]{3,2,1,0:T(8,128)S(1)}, u32[]{:S(2)}, u32[]{:S(2)}) collective-permute-start(f32[4,4,88,128]{3,2,1,0:T(8,128)S(1)} %get-tuple-element.23.own_in), channel_id=1, source_target_pairs={{0,1},{1,0},{2,3},{3,2},{4,5},{5,4},{6,7},{7,6},{8,9},{9,8},{10,11... | collective-permute-start | bytes 2162696 | tf_op jit(solution)/shard_map/ppermute | solution.py:480
  39.3 2.4 %collective-permute-start.5 = (f32[4,4,88,128]{3,2,1,0:T(8,128)S(1)}, f32[4,4,88,128]{3,2,1,0:T(8,128)S(1)}, u32[]{:S(2)}, u32[]{:S(2)}) collective-permute-start(f32[4,4,88,128]{3,2,1,0:T(8,128)S(1)} %get-tuple-element.23.own_in), channel_id=1, source_target_pairs={{1,2},{2,1},{3,4},{4,3},{5,6},{6,5},{9,10},{10,9},{11,12},{12,11},... | collective-permute-start | bytes 2162696 | tf_op jit(solution)/shard_map/ppermute | solution.py:483
  41.7 6.9 %collective-permute-done.11.off_in = f32[4,4,88,128]{3,2,1,0:T(8,128)S(1)} collective-permute-done((f32[4,4,88,128]{3,2,1,0:T(8,128)S(1)}, f32[4,4,88,128]{3,2,1,0:T(8,128)S(1)}, u32[]{:S(2)}, u32[]{:S(2)}) %collective-permute-start.11) | collective-permute-done | bytes 720928 | tf_op jit(solution)/shard_map/ppermute | solution.py:483
  48.6 5.4 %shard_map.69 = (f32[4,10,96,128]{3,2,1,0:T(8,128)S(1)}, f32[4,4,80,128]{3,2,1,0:T(8,128)S(1)}) custom-call(s32[1]{0:T(128)} %bitcast.parity_ref, f32[3,12,112,128]{3,2,1,0:T(8,128)S(1)} %get-tuple-element.18.coef_ref, f32[12,10,96,128]{3,2,1,0:T(8,128)S(1)} %get-tuple-element.19.inv_ref, f32[4,4,88,128]{3,2,1,0:T(8,128)S(1)} %get-tuple-element.26.own_in, ...), custom_call_target="tpu_custom_call" | custom-call | flops 5000000 | bytes 5000000 | tf_op jit(solution)/shard_map/pallas_call | solution.py:486
  54.1 0.4 collective-permute-start.12
  54.5 2.1 %collective-permute-start.13 = (f32[4,4,80,128]{3,2,1,0:T(8,128)S(1)}, f32[4,4,80,128]{3,2,1,0:T(8,128)S(1)}, u32[]{:S(2)}, u32[]{:S(2)}) collective-permute-start(f32[4,4,80,128]{3,2,1,0:T(8,128)S(1)} %get-tuple-element.27.own_in), channel_id=1, source_target_pairs={{1,2},{2,1},{3,4},{4,3},{5,6},{6,5},{9,10},{10,9},{11,12},{12,11},... | collective-permute-start | bytes 1966088 | tf_op jit(solution)/shard_map/ppermute | solution.py:483
  56.6 5.5 %shard_map.67 = (f32[4,10,96,128]{3,2,1,0:T(8,128)S(1)}, f32[4,4,80,128]{3,2,1,0:T(8,128)S(1)}) custom-call(s32[1]{0:T(128)} %bitcast.parity_ref, f32[3,12,112,128]{3,2,1,0:T(8,128)S(1)} %get-tuple-element.18.coef_ref, f32[12,10,96,128]{3,2,1,0:T(8,128)S(1)} %get-tuple-element.19.inv_ref, f32[4,4,88,128]{3,2,1,0:T(8,128)S(1)} %get-tuple-element.23.own_in, ...), custom_call_target="tpu_custom_call" | custom-call | flops 5000000 | bytes 5000000 | tf_op jit(solution)/shard_map/pallas_call | solution.py:486
  62.1 0.8 collective-permute-start.6
  62.9 2.7 %collective-permute-start.7 = (f32[4,4,80,128]{3,2,1,0:T(8,128)S(1)}, f32[4,4,80,128]{3,2,1,0:T(8,128)S(1)}, u32[]{:S(2)}, u32[]{:S(2)}) collective-permute-start(f32[4,4,80,128]{3,2,1,0:T(8,128)S(1)} %get-tuple-element.24.own_in), channel_id=1, source_target_pairs={{1,2},{2,1},{3,4},{4,3},{5,6},{6,5},{9,10},{10,9},{11,12},{12,11},... | collective-permute-start | bytes 1966088 | tf_op jit(solution)/shard_map/ppermute | solution.py:483
  65.6 0.8 collective-permute-done.13.off_in
  66.4 4.8 %shard_map.70.own_in = f32[4,4,72,128]{3,2,1,0:T(8,128)S(1)} custom-call(s32[1]{0:T(128)} %bitcast.parity_ref, f32[3,12,112,128]{3,2,1,0:T(8,128)S(1)} %get-tuple-element.18.coef_ref, f32[12,10,96,128]{3,2,1,0:T(8,128)S(1)} %get-tuple-element.19.inv_ref, f32[4,4,80,128]{3,2,1,0:T(8,128)S(1)} %get-tuple-element.27.own_in, ...), custom_call_target="tpu_custom_call" | custom-call | flops 5000000 | bytes 5000000 | tf_op jit(solution)/shard_map/pallas_call | solution.py:486
  71.2 0.2 collective-permute-start.14
  71.4 2.3 %collective-permute-start.15 = (f32[4,4,72,128]{3,2,1,0:T(8,128)S(1)}, f32[4,4,72,128]{3,2,1,0:T(8,128)S(1)}, u32[]{:S(2)}, u32[]{:S(2)}) collective-permute-start(f32[4,4,72,128]{3,2,1,0:T(8,128)S(1)} %shard_map.70.own_in), channel_id=1, source_target_pairs={{1,2},{2,1},{3,4},{4,3},{5,6},{6,5},{9,10},{10,9},{11,12},{12,11},... | collective-permute-start | bytes 1769480 | tf_op jit(solution)/shard_map/ppermute | solution.py:483
  73.7 1.1 collective-permute-done.7.off_in
  74.8 4.8 %shard_map.68.own_in = f32[4,4,72,128]{3,2,1,0:T(8,128)S(1)} custom-call(s32[1]{0:T(128)} %bitcast.parity_ref, f32[3,12,112,128]{3,2,1,0:T(8,128)S(1)} %get-tuple-element.18.coef_ref, f32[12,10,96,128]{3,2,1,0:T(8,128)S(1)} %get-tuple-element.19.inv_ref, f32[4,4,80,128]{3,2,1,0:T(8,128)S(1)} %get-tuple-element.24.own_in, ...), custom_call_target="tpu_custom_call" | custom-call | flops 5000000 | bytes 5000000 | tf_op jit(solution)/shard_map/pallas_call | solution.py:486
  79.5 0.2 collective-permute-start.8
  79.7 3.1 %collective-permute-start.9 = (f32[4,4,72,128]{3,2,1,0:T(8,128)S(1)}, f32[4,4,72,128]{3,2,1,0:T(8,128)S(1)}, u32[]{:S(2)}, u32[]{:S(2)}) collective-permute-start(f32[4,4,72,128]{3,2,1,0:T(8,128)S(1)} %shard_map.68.own_in), channel_id=1, source_target_pairs={{1,2},{2,1},{3,4},{4,3},{5,6},{6,5},{9,10},{10,9},{11,12},{12,11},... | collective-permute-start | bytes 1769480 | tf_op jit(solution)/shard_map/ppermute | solution.py:483
  82.8 4.9 %shard_map.71.rest_0_ = f32[8,4,64,128]{3,2,1,0:T(8,128)S(1)} custom-call(s32[1]{0:T(128)} %bitcast.parity_ref, f32[3,12,112,128]{3,2,1,0:T(8,128)S(1)} %get-tuple-element.18.coef_ref, f32[12,10,96,128]{3,2,1,0:T(8,128)S(1)} %get-tuple-element.19.inv_ref, f32[4,4,72,128]{3,2,1,0:T(8,128)S(1)} %shard_map.70.own_in, ...), custom_call_target="tpu_custom_call" | custom-call | flops 5000000 | bytes 5000000 | tf_op jit(solution)/shard_map/pallas_call | solution.py:486
  87.8 3.2 %collective-permute-done.9.off_in = f32[4,4,72,128]{3,2,1,0:T(8,128)S(1)} collective-permute-done((f32[4,4,72,128]{3,2,1,0:T(8,128)S(1)}, f32[4,4,72,128]{3,2,1,0:T(8,128)S(1)}, u32[]{:S(2)}, u32[]{:S(2)}) %collective-permute-start.9) | collective-permute-done | bytes 589856 | tf_op jit(solution)/shard_map/ppermute | solution.py:483
  90.9 4.9 %shard_map.72 = f32[8,4,64,128]{3,2,1,0:T(8,128)S(1)} custom-call(s32[1]{0:T(128)} %bitcast.parity_ref, f32[3,12,112,128]{3,2,1,0:T(8,128)S(1)} %get-tuple-element.18.coef_ref, f32[12,10,96,128]{3,2,1,0:T(8,128)S(1)} %get-tuple-element.19.inv_ref, f32[4,4,72,128]{3,2,1,0:T(8,128)S(1)} %shard_map.68.own_in, ...), custom_call_target="tpu_custom_call" | custom-call | flops 5000000 | bytes 5000000 | tf_op jit(solution)/shard_map/pallas_call | solution.py:486
  95.8 18.1 %all_to_all.10.back_ref = f32[4,2,4,64,128]{4,3,2,1,0:T(8,128)} all-to-all(f32[4,2,4,64,128]{4,3,2,1,0:T(8,128)S(1)} %bitcast.8), channel_id=1, replica_groups=mesh['tm'=4,'gx'=8] {'tm'}, dimensions={0} | all-to-all | bytes 2097152 | tf_op jit(solution)/shard_map/all_to_all | solution.py:582
  113.9 2.4 %finish.1 = f32[2,4,256,128]{3,2,1,0:T(8,128)} custom-call(f32[2]{0:T(128)} %weights_ref.3, f32[2,4,256,128]{3,2,1,0:T(8,128)} %state_ref.3, f32[4,2,4,64,128]{4,3,2,1,0:T(8,128)} %all_to_all.10.back_ref), custom_call_target="tpu_custom_call" | custom-call | tf_op jit(solution)/shard_map/finish/pallas_call | solution.py:589
  (23 shorter events, 0.3 us)
Async XLA Ops:
  2.3 3.9 %copy-start.2 = (f32[4,256,128]{2,1,0:T(8,128)S(1)}, f32[4,256,128]{2,1,0:T(8,128)}, u32[]{:S(2)}) copy-start(f32[4,256,128]{2,1,0:T(8,128)} %param.7) | copy-start | bytes 1572868
  2.3 3.9 %copy-start.3 = (f32[4,256,128]{2,1,0:T(8,128)S(1)}, f32[4,256,128]{2,1,0:T(8,128)}, u32[]{:S(2)}) copy-start(f32[4,256,128]{2,1,0:T(8,128)} %param.8) | copy-start | bytes 1572868
  2.3 23.2 %all-to-all-start = ((f32[4,2,4,96,128]{4,3,2,1,0:T(8,128)}), f32[4,2,4,96,128]{4,3,2,1,0:T(8,128)S(1)}, u32[]{:S(2)}, u32[]{:S(2)}) async-start(f32[4,2,4,96,128]{4,3,2,1,0:T(8,128)} %pack.1), calls=%async_computation | async-start | bytes 3145728 | tf_op jit(solution)/shard_map/all_to_all | solution.py:510
  6.1 22.0 %copy-start = (f32[8]{0:T(128)S(1)}, f32[8]{0:T(128)}, u32[]{:S(2)}) copy-start(f32[8]{0:T(128)} %shift_real_ref.1) | copy-start | bytes 100
  6.1 22.0 %copy-start.1 = (f32[8]{0:T(128)S(1)}, f32[8]{0:T(128)}, u32[]{:S(2)}) copy-start(f32[8]{0:T(128)} %shift_imag_ref.1) | copy-start | bytes 100
  6.2 21.9 %collective-permute-start.1 = (f32[2,4,96,128]{3,2,1,0:T(8,128)S(1)}, f32[2,4,96,128]{3,2,1,0:T(8,128)S(1)}, u32[]{:S(2)}, u32[]{:S(2)}) collective-permute-start(f32[2,4,96,128]{3,2,1,0:T(8,128)S(1)} %fusion.1.fixed_own), channel_id=1, source_target_pairs={{0,1},{1,0},{2,3},{3,2},{4,5},{5,4},{6,7},{7,6},{8,9},{9,8},{10,11... | collective-permute-start | bytes 1179656 | tf_op jit(solution)/shard_map/ppermute | solution.py:480
  6.3 21.8 %collective-permute-start.2 = (f32[2,4,96,128]{3,2,1,0:T(8,128)S(1)}, f32[2,4,96,128]{3,2,1,0:T(8,128)S(1)}, u32[]{:S(2)}, u32[]{:S(2)}) collective-permute-start(f32[2,4,96,128]{3,2,1,0:T(8,128)S(1)} %fusion.1.fixed_own), channel_id=1, source_target_pairs={{1,2},{2,1},{3,4},{4,3},{5,6},{6,5},{9,10},{10,9},{11,12},{12,11},... | collective-permute-start | bytes 1179656 | tf_op jit(solution)/shard_map/ppermute | solution.py:483
  25.6 2.6 %collective-permute-start = (f32[8,1,96,128]{3,2,1,0:T(8,128)S(1)}, f32[8,1,96,128]{3,2,1,0:T(8,128)S(1)}, u32[]{:S(2)}, u32[]{:S(2)}) collective-permute-start(f32[8,1,96,128]{3,2,1,0:T(8,128)S(1)} %get-tuple-element.17), channel_id=1, source_target_pairs={{0,1},{1,0},{2,3},{3,2},{4,5},{5,4},{6,7},{7,6},{8,9},{9,8},{10,11... | collective-permute-start | bytes 1179656 | tf_op jit(solution)/shard_map/ppermute | solution.py:480
  25.6 9.1 %collective-permute-start.3 = (f32[8,1,96,128]{3,2,1,0:T(8,128)S(1)}, f32[8,1,96,128]{3,2,1,0:T(8,128)S(1)}, u32[]{:S(2)}, u32[]{:S(2)}) collective-permute-start(f32[8,1,96,128]{3,2,1,0:T(8,128)S(1)} %get-tuple-element.20), channel_id=1, source_target_pairs={{1,2},{2,1},{3,4},{4,3},{5,6},{6,5},{9,10},{10,9},{11,12},{12,11},... | collective-permute-start | bytes 1179656 | tf_op jit(solution)/shard_map/ppermute | solution.py:483
  35.5 6.2 %collective-permute-start.10 = (f32[4,4,88,128]{3,2,1,0:T(8,128)S(1)}, f32[4,4,88,128]{3,2,1,0:T(8,128)S(1)}, u32[]{:S(2)}, u32[]{:S(2)}) collective-permute-start(f32[4,4,88,128]{3,2,1,0:T(8,128)S(1)} %get-tuple-element.26.own_in), channel_id=1, source_target_pairs={{0,1},{1,0},{2,3},{3,2},{4,5},{5,4},{6,7},{7,6},{8,9},{9,8},{10,11... | collective-permute-start | bytes 2162696 | tf_op jit(solution)/shard_map/ppermute | solution.py:480
  36.0 12.6 %collective-permute-start.11 = (f32[4,4,88,128]{3,2,1,0:T(8,128)S(1)}, f32[4,4,88,128]{3,2,1,0:T(8,128)S(1)}, u32[]{:S(2)}, u32[]{:S(2)}) collective-permute-start(f32[4,4,88,128]{3,2,1,0:T(8,128)S(1)} %get-tuple-element.26.own_in), channel_id=1, source_target_pairs={{1,2},{2,1},{3,4},{4,3},{5,6},{6,5},{9,10},{10,9},{11,12},{12,11},... | collective-permute-start | bytes 2162696 | tf_op jit(solution)/shard_map/ppermute | solution.py:483
  38.0 18.6 %collective-permute-start.4 = (f32[4,4,88,128]{3,2,1,0:T(8,128)S(1)}, f32[4,4,88,128]{3,2,1,0:T(8,128)S(1)}, u32[]{:S(2)}, u32[]{:S(2)}) collective-permute-start(f32[4,4,88,128]{3,2,1,0:T(8,128)S(1)} %get-tuple-element.23.own_in), channel_id=1, source_target_pairs={{0,1},{1,0},{2,3},{3,2},{4,5},{5,4},{6,7},{7,6},{8,9},{9,8},{10,11... | collective-permute-start | bytes 2162696 | tf_op jit(solution)/shard_map/ppermute | solution.py:480
  39.3 17.4 %collective-permute-start.5 = (f32[4,4,88,128]{3,2,1,0:T(8,128)S(1)}, f32[4,4,88,128]{3,2,1,0:T(8,128)S(1)}, u32[]{:S(2)}, u32[]{:S(2)}) collective-permute-start(f32[4,4,88,128]{3,2,1,0:T(8,128)S(1)} %get-tuple-element.23.own_in), channel_id=1, source_target_pairs={{1,2},{2,1},{3,4},{4,3},{5,6},{6,5},{9,10},{10,9},{11,12},{12,11},... | collective-permute-start | bytes 2162696 | tf_op jit(solution)/shard_map/ppermute | solution.py:483
  54.1 11.5 %collective-permute-start.12 = (f32[4,4,80,128]{3,2,1,0:T(8,128)S(1)}, f32[4,4,80,128]{3,2,1,0:T(8,128)S(1)}, u32[]{:S(2)}, u32[]{:S(2)}) collective-permute-start(f32[4,4,80,128]{3,2,1,0:T(8,128)S(1)} %get-tuple-element.27.own_in), channel_id=1, source_target_pairs={{0,1},{1,0},{2,3},{3,2},{4,5},{5,4},{6,7},{7,6},{8,9},{9,8},{10,11... | collective-permute-start | bytes 1966088 | tf_op jit(solution)/shard_map/ppermute | solution.py:480
  54.5 11.9 %collective-permute-start.13 = (f32[4,4,80,128]{3,2,1,0:T(8,128)S(1)}, f32[4,4,80,128]{3,2,1,0:T(8,128)S(1)}, u32[]{:S(2)}, u32[]{:S(2)}) collective-permute-start(f32[4,4,80,128]{3,2,1,0:T(8,128)S(1)} %get-tuple-element.27.own_in), channel_id=1, source_target_pairs={{1,2},{2,1},{3,4},{4,3},{5,6},{6,5},{9,10},{10,9},{11,12},{12,11},... | collective-permute-start | bytes 1966088 | tf_op jit(solution)/shard_map/ppermute | solution.py:483
  62.1 11.6 %collective-permute-start.6 = (f32[4,4,80,128]{3,2,1,0:T(8,128)S(1)}, f32[4,4,80,128]{3,2,1,0:T(8,128)S(1)}, u32[]{:S(2)}, u32[]{:S(2)}) collective-permute-start(f32[4,4,80,128]{3,2,1,0:T(8,128)S(1)} %get-tuple-element.24.own_in), channel_id=1, source_target_pairs={{0,1},{1,0},{2,3},{3,2},{4,5},{5,4},{6,7},{7,6},{8,9},{9,8},{10,11... | collective-permute-start | bytes 1966088 | tf_op jit(solution)/shard_map/ppermute | solution.py:480
  62.9 11.9 %collective-permute-start.7 = (f32[4,4,80,128]{3,2,1,0:T(8,128)S(1)}, f32[4,4,80,128]{3,2,1,0:T(8,128)S(1)}, u32[]{:S(2)}, u32[]{:S(2)}) collective-permute-start(f32[4,4,80,128]{3,2,1,0:T(8,128)S(1)} %get-tuple-element.24.own_in), channel_id=1, source_target_pairs={{1,2},{2,1},{3,4},{4,3},{5,6},{6,5},{9,10},{10,9},{11,12},{12,11},... | collective-permute-start | bytes 1966088 | tf_op jit(solution)/shard_map/ppermute | solution.py:483
  71.2 11.7 %collective-permute-start.14 = (f32[4,4,72,128]{3,2,1,0:T(8,128)S(1)}, f32[4,4,72,128]{3,2,1,0:T(8,128)S(1)}, u32[]{:S(2)}, u32[]{:S(2)}) collective-permute-start(f32[4,4,72,128]{3,2,1,0:T(8,128)S(1)} %shard_map.70.own_in), channel_id=1, source_target_pairs={{0,1},{1,0},{2,3},{3,2},{4,5},{5,4},{6,7},{7,6},{8,9},{9,8},{10,11... | collective-permute-start | bytes 1769480 | tf_op jit(solution)/shard_map/ppermute | solution.py:480
  71.4 11.5 %collective-permute-start.15 = (f32[4,4,72,128]{3,2,1,0:T(8,128)S(1)}, f32[4,4,72,128]{3,2,1,0:T(8,128)S(1)}, u32[]{:S(2)}, u32[]{:S(2)}) collective-permute-start(f32[4,4,72,128]{3,2,1,0:T(8,128)S(1)} %shard_map.70.own_in), channel_id=1, source_target_pairs={{1,2},{2,1},{3,4},{4,3},{5,6},{6,5},{9,10},{10,9},{11,12},{12,11},... | collective-permute-start | bytes 1769480 | tf_op jit(solution)/shard_map/ppermute | solution.py:483
  79.5 8.2 %collective-permute-start.8 = (f32[4,4,72,128]{3,2,1,0:T(8,128)S(1)}, f32[4,4,72,128]{3,2,1,0:T(8,128)S(1)}, u32[]{:S(2)}, u32[]{:S(2)}) collective-permute-start(f32[4,4,72,128]{3,2,1,0:T(8,128)S(1)} %shard_map.68.own_in), channel_id=1, source_target_pairs={{0,1},{1,0},{2,3},{3,2},{4,5},{5,4},{6,7},{7,6},{8,9},{9,8},{10,11... | collective-permute-start | bytes 1769480 | tf_op jit(solution)/shard_map/ppermute | solution.py:480
  79.7 11.2 %collective-permute-start.9 = (f32[4,4,72,128]{3,2,1,0:T(8,128)S(1)}, f32[4,4,72,128]{3,2,1,0:T(8,128)S(1)}, u32[]{:S(2)}, u32[]{:S(2)}) collective-permute-start(f32[4,4,72,128]{3,2,1,0:T(8,128)S(1)} %shard_map.68.own_in), channel_id=1, source_target_pairs={{1,2},{2,1},{3,4},{4,3},{5,6},{6,5},{9,10},{10,9},{11,12},{12,11},... | collective-permute-start | bytes 1769480 | tf_op jit(solution)/shard_map/ppermute | solution.py:483
